TPU v7x, 32 devices: a whole 2x2x4 slice. The times are simulated.
32 devices in a mesh: gz: 4 (over x, core), gy: 8 (over z, y).
Axes of the slice: x: 2, y: 2, z: 4, core: 2. Of those that a mesh axis runs over, the one named last changes fastest.
Arguments:
- distance: float32 [256, 128, 1024], P('gz', 'gy'), may hold values from 0 to 2
- parent: int32 [256, 128, 1024], P('gz', 'gy'), may hold values from 0 to 4095, as said below
- removed: int32 [4096], replicated, may hold values from 0 to 1
- occupied: int32 [256, 128, 1024], P('gz', 'gy'), may hold values 0 or 1
Outputs:
- lowered: float32 [256, 128, 1024], P('gz', 'gy')
- cleared_share: float32 [], replicated
Inputs may be any that keep to these rules, and one draw needn't show every extreme that they name: `parent`: an obstacle id.
All inputs are finite; a program needn't handle non-finite values. No bound on the sum of `occupied` on one device may be relied on, other than what follows from the above.
Results may differ from a plain program's by a relative error of at most 0.0003.
Values sent between devices are 32-bit elements; how exact they have to be, the bound alone decides.
No kernel may reach another device: no remote copies, remote signals or barrier semaphores. Data moves between devices by JAX's collectives and lax.ppermute only.
A program may use at most 64 MiB of HBM per device.

v0:
```python
import functools

import jax
import jax.numpy as jnp
from jax import lax
from jax.experimental import pallas as pl
from jax.experimental.pallas import tpu as pltpu
from jax.sharding import PartitionSpec as P


FAR = 1000000.0
VOXEL = 0.1
TRUNC = 2.0
LANES = 128
SUBLANES = 8
CHUNK = 8
READ = 8
AHEAD = 3
RAISE_UNROLL = 8
SWEEP_UNROLL = 8
MIB = 2**20

HBM = pl.BlockSpec(memory_space=pltpu.HBM)
VMEM = pl.BlockSpec(memory_space=pltpu.VMEM)

COUNT_BITS = 12


def params(mib):
    return pltpu.CompilerParams(vmem_limit_bytes=mib * MIB)


def cost(mib):
    return pl.CostEstimate(flops=0, bytes_accessed=mib * MIB, transcendentals=0)


def packed_table(flags_ref):
    bits = (flags_ref[...] == 1).astype(jnp.int32)
    bits = bits << lax.broadcasted_iota(jnp.int32, bits.shape, 0)
    words = jnp.sum(bits, axis=0, keepdims=True)
    return jnp.broadcast_to(words, (SUBLANES, LANES))


PICK = lax.GatherDimensionNumbers(
    offset_dims=(),
    collapsed_slice_dims=(1,),
    start_index_map=(1,),
    operand_batching_dims=(0,),
    start_indices_batching_dims=(0,),
)


def raise_tile(words, dist, par, occ):
    lane = par & (LANES - 1)
    word = lax.gather(words, lane[..., None], PICK, (1, 1), mode="promise_in_bounds")
    cleared = (word >> (par >> 7)) & (occ ^ 1)
    raised = jnp.where(occ == 1, 0.0, jnp.where(cleared == 1, TRUNC, dist))
    return raised, cleared


def swept_tiles(centers, others):
    lane = lax.broadcasted_iota(jnp.int32, (SUBLANES, LANES), 1)
    last = len(centers) - 1
    after = [pltpu.roll(c, 1, 1) for c in centers]
    before = [pltpu.roll(c, LANES - 1, 1) for c in centers]
    swept = []
    for i, center in enumerate(centers):
        left = jnp.where(lane == 0, after[i - 1] if i else FAR, after[i])
        right = jnp.where(lane == LANES - 1, before[i + 1] if i < last else FAR, before[i])
        nearest = jnp.minimum(left, right)
        for other in others[i]:
            nearest = jnp.minimum(nearest, other)
        swept.append(jnp.minimum(center, nearest + VOXEL))
    return swept


def padded_rows(rows, cols):
    return cols // LANES * (rows + SUBLANES) + SUBLANES


def row_of(column, row, rows):
    return column * (rows + SUBLANES) + SUBLANES + row


def fill_pads(ref, at, rows, cols):
    for column in range(cols // LANES + 1):
        first = row_of(column, -SUBLANES, rows)
        ref[(*at, pl.ds(first, SUBLANES), slice(None))] = jnp.full((SUBLANES, LANES), FAR)


def swept_plane(read, rows, cols, y, beside=(-1, 1)):
    firsts = [row_of(c, y, rows) for c in range(cols // LANES)]
    centers = [read(0, f) for f in firsts]
    others = [[read(dz, f) for dz in beside] + [read(0, f - 1), read(0, f + 1)] for f in firsts]
    return swept_tiles(centers, others)


def face_tiles(field, rows, cols, row, inward, z):
    planes, height, _ = field.shape
    lines = field.reshape(planes * height, LANES)
    columns = range(cols // LANES)

    def read(column, y, dz=0):
        first = (z + 1 + dz) * height + row_of(column, y, rows)
        return lines[pl.ds(first, SUBLANES, stride=height), :]

    ends = [read(c, row) for c in columns]
    others = [(read(c, row, -1), read(c, row, 1), read(c, inward)) for c in columns]
    return ends, swept_tiles(ends, others)


def write_faces(field, rows, cols, top, start, out):
    def body(group, _):
        at = pl.ds(pl.multiple_of(group * SUBLANES, SUBLANES), SUBLANES)

        def write(row, inward):
            ends, swept = face_tiles(field, rows, cols, row, inward, start + group * SUBLANES)
            for column, (end, tile) in enumerate(zip(ends, swept)):
                x = pl.ds(column * LANES, LANES)
                out[0, at, x] = end
                out[1, at, x] = tile

        pl.when(top)(lambda: write(rows - 1, rows - 2))
        pl.when(jnp.logical_not(top))(lambda: write(0, 1))
        return 0

    lax.fori_loop(0, out.shape[1] // SUBLANES, body, 0)


def faces_kernel(rows, cols, toward_odd, field, out):
    odd = lax.axis_index("gy") & 1
    write_faces(field, rows, cols, odd == toward_odd, 0, out)


def faces(field, rows, cols, toward_odd):
    return pl.pallas_call(
        functools.partial(faces_kernel, rows, cols, toward_odd),
        out_shape=jax.ShapeDtypeStruct((2, field.shape[0] - 2, cols), jnp.float32),
        in_specs=[VMEM],
        out_specs=VMEM,
        compiler_params=params(4),
        cost_estimate=cost(2),
    )(field)


def raise_planes(start, count, dist, par, flags_at, occ, field, flags, buf, fsem, sem):
    _, rows, cols = dist.shape
    columns = range(cols // LANES)
    chunks = count // READ

    def reads(chunk):
        source, target = pl.ds(start + chunk * READ, READ), pl.ds(chunk * READ, READ)
        return [
            pltpu.make_async_copy(src.at[source], dst.at[target], sem.at[which, chunk])
            for which, (src, dst) in enumerate(zip((dist, par, occ), buf))
        ]

    table_in = pltpu.make_async_copy(flags_at, flags, fsem)
    table_in.start()
    for chunk in range(min(AHEAD, chunks)):
        for cp in reads(chunk):
            cp.start()
    for z in (0, field.shape[0] - 1):
        if start < z <= start + count + 1 or z == start == 0:
            field[z] = jnp.full(field.shape[1:], FAR)
    table_in.wait()
    table = packed_table(flags)

    def body(chunk, acc):
        @pl.when(chunk + AHEAD < chunks)
        def _():
            for cp in reads(chunk + AHEAD):
                cp.start()

        for cp in reads(chunk):
            cp.wait()

        def planes(group, acc):
            for part in range(RAISE_UNROLL):
                z = chunk * READ + group * RAISE_UNROLL + part
                fill_pads(field, (start + z + 1,), rows, cols)
                for y in range(0, rows, SUBLANES):
                    for column in columns:
                        at = (z, pl.ds(y, SUBLANES), pl.ds(column * LANES, LANES))
                        tile, cleared = raise_tile(table, *(b[at] for b in buf))
                        to = pl.ds(row_of(column, y, rows), SUBLANES)
                        field[start + z + 1, to, :] = tile
                        acc[part] = acc[part] + cleared
            return acc

        return lax.fori_loop(0, READ // RAISE_UNROLL, planes, acc)

    zeros = jnp.zeros((SUBLANES, LANES), jnp.int32)
    parts = lax.fori_loop(0, chunks, body, [zeros] * RAISE_UNROLL)
    return sum(parts[1:], parts[0])


def keep_end(field, z, inward, rows, cols, out):
    def read(dz, at):
        return field[z + 1 + dz, pl.ds(at, SUBLANES), :]

    for y in range(0, rows, SUBLANES):
        swept = swept_plane(read, rows, cols, y, (inward,))
        for column in range(cols // LANES):
            x = pl.ds(column * LANES, LANES)
            out[pl.ds(y, SUBLANES), x] = read(0, row_of(column, y, rows))
            out[pl.ds(rows + y, SUBLANES), x] = swept[column]


def raise_kernel(dist, par, flags_at, occ, field, first, second, flags, buf, ends, fsem, sem):
    depth, rows, cols = dist.shape
    total = raise_planes(0, depth, dist, par, flags_at, occ, field, flags, buf, fsem, sem)
    keep_end(field, 0, 1, rows, cols, ends.at[0])
    keep_end(field, depth - 1, -1, rows, cols, ends.at[1])
    count = jnp.sum(total)
    row = lax.broadcasted_iota(jnp.int32, (SUBLANES, cols), 0)
    small = (count & (2**COUNT_BITS - 1)).astype(jnp.float32)
    large = (count >> COUNT_BITS).astype(jnp.float32)
    counts = jnp.where(row == 2, small, jnp.where(row == 3, large, 0.0))
    odd = lax.axis_index("gz") & 1
    for out, side in ((first, odd), (second, 1 - odd)):
        out[pl.ds(0, 2 * rows), :] = ends[side]
        out[pl.ds(2 * rows, SUBLANES), :] = counts


def raise_scratch(count, dist, par, flags, occ):
    return [
        pltpu.VMEM(flags.shape, jnp.int32),
        [pltpu.VMEM((count, *a.shape[1:]), a.dtype) for a in (dist, par, occ)],
        pltpu.SemaphoreType.DMA,
        pltpu.SemaphoreType.DMA((3, count // READ)),
    ]


def raise_all(dist, par, flags, occ):
    depth, rows, cols = dist.shape
    message = jax.ShapeDtypeStruct((2 * rows + SUBLANES, cols), jnp.float32)
    scratch = raise_scratch(depth, dist, par, flags, occ)
    return pl.pallas_call(
        raise_kernel,
        name="raise_all",
        out_shape=(
            jax.ShapeDtypeStruct((depth + 2, padded_rows(rows, cols), LANES), jnp.float32),
            message,
            message,
        ),
        in_specs=[HBM] * 4,
        out_specs=(VMEM,) * 3,
        scratch_shapes=scratch[:2] + [pltpu.VMEM((2, 2 * rows, cols), jnp.float32)] + scratch[2:],
        compiler_params=params(20),
        cost_estimate=cost(12),
    )(dist, par, flags, occ)


def sweep_once_kernel(start, count, rows, cols, field, once):
    depth = field.shape[0] - 2

    def sweep(z):
        def read(dz, at):
            return field[z + 1 + dz, pl.ds(at, SUBLANES), :]

        fill_pads(once, (z - start + 1,), rows, cols)
        for y in range(0, rows, SUBLANES):
            for column, tile in enumerate(swept_plane(read, rows, cols, y)):
                once[z - start + 1, pl.ds(row_of(column, y, rows), SUBLANES), :] = tile

    def body(group, _):
        for part in range(SWEEP_UNROLL):
            sweep(start + group * SWEEP_UNROLL + part)
        return 0

    for z in (start - 1, start + count):
        if 0 <= z < depth:
            sweep(z)
        else:
            once[z - start + 1] = jnp.full(once.shape[1:], FAR)
    lax.fori_loop(0, count // SWEEP_UNROLL, body, 0)


def sweep_once(field, start, count, rows, cols):
    return pl.pallas_call(
        functools.partial(sweep_once_kernel, start, count, rows, cols),
        out_shape=jax.ShapeDtypeStruct((count + 2, *field.shape[1:]), jnp.float32),
        in_specs=[VMEM],
        out_specs=VMEM,
        compiler_params=params(8),
        cost_estimate=cost(8),
    )(field)


def sweep_again_planes(once, first, count, tiles, slab):
    _, rows, cols = tiles.shape
    columns = range(cols // LANES)

    def body(group, _):
        for part in range(SWEEP_UNROLL):
            plane = first + group * SWEEP_UNROLL + part

            def read(dz, at):
                return once[plane + 1 + dz, pl.ds(at, SUBLANES), :]

            for y in range(0, rows, SUBLANES):
                for column, tile in enumerate(swept_plane(read, rows, cols, y)):
                    tiles[plane, pl.ds(y, SUBLANES), pl.ds(column * LANES, LANES)] = tile
                    at = plane * (rows * len(columns)) + column * rows + y
                    slab[pl.ds(pl.multiple_of(at, SUBLANES), SUBLANES), :] = tile
        return 0

    lax.fori_loop(0, count // SWEEP_UNROLL, body, 0)


def sweep_again_low_kernel(once, tiles, slab):
    sweep_again_planes(once, 0, tiles.shape[0], tiles, slab)


def sweep_again_high_kernel(once, low, out, slab, tiles, sem):
    half = low.shape[0]
    copies = [pltpu.make_async_copy(low, out.at[pl.ds(0, half)], sem.at[0])]
    copies[0].start()
    for step, first in enumerate(range(0, tiles.shape[0], CHUNK)):
        sweep_again_planes(once, first, CHUNK, tiles, slab)
        at = pl.ds(first, CHUNK)
        to = out.at[pl.ds(half + first, CHUNK)]
        cp = pltpu.make_async_copy(tiles.at[at], to, sem.at[step + 1])
        cp.start()
        copies.append(cp)
    for cp in copies:
        cp.wait()


def sweep_again_low(once, rows, cols):
    count = once.shape[0] - 2
    return pl.pallas_call(
        sweep_again_low_kernel,
        name="sweep_again_low",
        out_shape=(
            jax.ShapeDtypeStruct((count, rows, cols), jnp.float32),
            jax.ShapeDtypeStruct((count * rows * cols // LANES, LANES), jnp.float32),
        ),
        in_specs=[VMEM],
        out_specs=(VMEM, VMEM),
        compiler_params=params(4),
        cost_estimate=cost(8),
    )(once)


def sweep_again_high(once, low):
    count = once.shape[0] - 2
    _, rows, cols = low.shape
    return pl.pallas_call(
        sweep_again_high_kernel,
        name="sweep_again_high",
        out_shape=(
            jax.ShapeDtypeStruct((low.shape[0] + count, rows, cols), jnp.float32),
            jax.ShapeDtypeStruct((count * rows * cols // LANES, LANES), jnp.float32),
        ),
        in_specs=[VMEM, VMEM],
        out_specs=(HBM, VMEM),
        scratch_shapes=[
            pltpu.VMEM((count, rows, cols), jnp.float32),
            pltpu.SemaphoreType.DMA((count // CHUNK + 1,)),
        ],
        compiler_params=params(8),
        cost_estimate=cost(8),
    )(once, low)


def corners_kernel(first, second, counts, more, low, high, total):
    rows = (first.shape[0] - SUBLANES) // 2
    odd = lax.axis_index("gz") & 1
    total[...] = counts[...] + more[...]
    low[...] = total[...]
    high[...] = total[...]
    for side in range(2):
        for out, row in ((low, 0), (high, rows - 1)):
            line = jnp.where(odd == side, first[pl.ds(row, 1), :], second[pl.ds(row, 1), :])
            out[pl.ds(side, 1), :] = line


def corners(first, second, counts, more):
    shape = jax.ShapeDtypeStruct(counts.shape, jnp.float32)
    return pl.pallas_call(
        corners_kernel,
        name="corners",
        out_shape=(shape,) * 3,
        in_specs=[VMEM] * 4,
        out_specs=(VMEM,) * 3,
        compiler_params=params(2),
        cost_estimate=cost(1),
    )(first, second, counts, more)


def patch_z_kernel(slabs, first, second, slab_low, slab_high, _, out, edges, planes, sem):
    depth, rows, cols = out.shape
    columns = range(cols // LANES)
    slab = lax.axis_index("gz")
    odd = slab & 1
    size = rows * len(columns)
    stores = []
    for side, own in enumerate((slab_low, slab_high)):
        missing = slab == (0, slabs - 1)[side]
        base = (0, own.shape[0] - 2 * size)[side]
        for away in range(2):
            plane = (away, 1 - away)[side]
            offered = (rows, 0)[away]
            for y in range(0, rows, SUBLANES):
                for column in columns:
                    x = pl.ds(column * LANES, LANES)
                    at = (pl.ds(offered + y, SUBLANES), x)
                    got = jnp.where(odd == side, first[at], second[at])
                    got = jnp.where(missing, FAR, got) + VOXEL
                    if away:
                        got = got + VOXEL
                    tile = own[pl.ds(base + plane * size + column * rows + y, SUBLANES), :]
                    planes[side, plane, pl.ds(y, SUBLANES), x] = jnp.minimum(tile, got)
        to = out.at[pl.ds((0, depth - 2)[side], 2)]
        cp = pltpu.make_async_copy(planes.at[side], to, sem.at[side])
        cp.start()
        stores.append(cp)
    for edge, row in enumerate((0, 1, rows - 2, rows - 1)):
        z = 0
        for own in (slab_low, slab_high):
            for base in range(0, own.shape[0], SUBLANES * size):
                for column in columns:
                    tile = own[pl.ds(base + column * rows + row, SUBLANES, stride=size), :]
                    edges[edge, pl.ds(z, SUBLANES), pl.ds(column * LANES, LANES)] = tile
                z += SUBLANES
        for side in range(2):
            for plane in range(2):
                at = pl.ds((0, depth - 2)[side] + plane, 1)
                edges[edge, at, :] = planes[side, plane, pl.ds(row, 1), :]
    for cp in stores:
        cp.wait()


def patch_z(first, second, slab_low, slab_high, out):
    depth, rows, cols = out.shape
    return pl.pallas_call(
        functools.partial(patch_z_kernel, lax.axis_size("gz")),
        name="patch_z",
        out_shape=(
            jax.ShapeDtypeStruct(out.shape, out.dtype),
            jax.ShapeDtypeStruct((4, depth, cols), jnp.float32),
        ),
        in_specs=[VMEM] * 4 + [HBM],
        out_specs=(HBM, VMEM),
        input_output_aliases={4: 0},
        scratch_shapes=[
            pltpu.VMEM((2, 2, rows, cols), jnp.float32),
            pltpu.SemaphoreType.DMA((2,)),
        ],
        compiler_params=params(4),
        cost_estimate=cost(1),
    )(first, second, slab_low, slab_high, out)


def merge_rows(away, edges, face, corner, missing, buf):
    reach = face[1 - away] + VOXEL
    if away:
        reach = reach + VOXEL
    buf[...] = jnp.minimum(edges[...], reach)
    if corner is not None:
        for end, z in enumerate((0, buf.shape[0] - 1)):
            offer = jnp.where(missing[end], FAR, corner[pl.ds(end, 1), :])
            line = pl.ds(z, 1)
            buf[line, :] = jnp.minimum(buf[line, :], offer + VOXEL + VOXEL)


def sides(rows):
    return (((0, 0), (1, 1)), ((rows - 1, 3), (rows - 2, 2)))


def patch_near_kernel(edges, near, _, out, buf, sem):
    odd = lax.axis_index("gy") & 1
    for side, places in enumerate(sides(out.shape[1])):

        @pl.when(odd == side)
        def _():
            copies = []
            for away, (row, edge) in enumerate(places):
                merge_rows(away, edges.at[edge], near, None, None, buf.at[away])
                cp = pltpu.make_async_copy(buf.at[away], out.at[:, row, :], sem.at[away])
                cp.start()
                copies.append(cp)
            for cp in copies:
                cp.wait()


def patch_far_kernel(
    scale, slabs, edges, near, far, clow, chigh, counts, _, out, share, buf, lines, sem
):
    depth, rows, _ = out.shape
    odd = lax.axis_index("gy") & 1
    slab = lax.axis_index("gz")
    missing = (slab == 0, slab == slabs - 1)
    corners = (clow, chigh)
    for side, places in enumerate(sides(rows)):

        @pl.when(odd == 1 - side)
        def _():
            copies = []
            for away, (row, edge) in enumerate(places):
                corner = None if away else corners[side]
                merge_rows(away, edges.at[edge], far, corner, missing, buf.at[away])
                cp = pltpu.make_async_copy(buf.at[away], out.at[:, row, :], sem.at[away])
                cp.start()
                copies.append(cp)
            row, edge = sides(rows)[1 - side][0]
            for end, z in enumerate((0, depth - 1)):
                line = pl.ds(z, 1)
                reach = jnp.minimum(edges[edge, line, :], near[1, line, :] + VOXEL)
                offer = jnp.where(missing[end], FAR, corners[1 - side][pl.ds(end, 1), :])
                lines[end] = jnp.minimum(reach, offer + VOXEL + VOXEL)
                cp = pltpu.make_async_copy(
                    lines.at[end], out.at[line, row, :], sem.at[2 + end]
                )
                cp.start()
                copies.append(cp)
            for cp in copies:
                cp.wait()

    x = pl.ds(0, LANES)
    both = (counts[:, x] + clow[:, x]).astype(jnp.int32)
    row = lax.broadcasted_iota(jnp.int32, both.shape, 0)
    both = jnp.where(row == 2, both, jnp.where(row == 3, both << COUNT_BITS, 0))
    count = jnp.sum(both, axis=0, keepdims=True)
    share[...] = count[:, :1].astype(jnp.float32) * jnp.float32(scale)


def patch_near(edges, near, out):
    depth, _, cols = out.shape
    return pl.pallas_call(
        patch_near_kernel,
        name="patch_near",
        out_shape=jax.ShapeDtypeStruct(out.shape, out.dtype),
        in_specs=[VMEM] * 2 + [HBM],
        out_specs=HBM,
        input_output_aliases={2: 0},
        scratch_shapes=[pltpu.VMEM((2, depth, cols), jnp.float32), pltpu.SemaphoreType.DMA((2,))],
        compiler_params=params(4),
        cost_estimate=cost(1),
    )(edges, near, out)


def patch_far(scale, edges, near, far, clow, chigh, counts, out):
    depth, _, cols = out.shape
    return pl.pallas_call(
        functools.partial(patch_far_kernel, scale, lax.axis_size("gz")),
        name="patch_far",
        out_shape=(
            jax.ShapeDtypeStruct(out.shape, out.dtype),
            jax.ShapeDtypeStruct((1, 1), jnp.float32),
        ),
        in_specs=[VMEM] * 6 + [HBM],
        out_specs=(HBM, VMEM),
        input_output_aliases={6: 0},
        scratch_shapes=[
            pltpu.VMEM((2, depth, cols), jnp.float32),
            pltpu.VMEM((2, 1, cols), jnp.float32),
            pltpu.SemaphoreType.DMA((4,)),
        ],
        compiler_params=params(4),
        cost_estimate=cost(1),
    )(edges, near, far, clow, chigh, counts, out)


def swapped(value, axis, partner):
    count = lax.axis_size(axis)
    return lax.ppermute(value, axis, [(i, partner(i) % count) for i in range(count)])


def after_odd(i):
    return i - 1 + 2 * (i % 2)


def shifted(value, axis, by):
    return swapped(value, axis, lambda i: i + by)


def on_device(distance, parent, removed, occupied):
    depth, rows, cols = distance.shape
    half = depth // 2
    slabs, columns = lax.axis_size("gz"), lax.axis_size("gy")
    tied = lax.optimization_barrier
    distance, parent, flags, occupied = (
        pltpu.with_memory_space_constraint(a, pltpu.HBM)
        for a in (distance, parent, removed.reshape(-1, LANES), occupied)
    )
    field, first, second = raise_all(distance, parent, flags, occupied)
    face0 = faces(field, rows, cols, 1)
    near = swapped(face0, "gy", after_odd)
    got_first = swapped(first, "gz", after_odd)
    face1 = faces(field, rows, cols, 0)
    once0 = sweep_once(field, 0, half, rows, cols)
    got_first, once0 = tied((got_first, once0))
    second = second.at[2 * rows :].add(got_first[2 * rows :])
    got_second = swapped(second, "gz", lambda i: i ^ 1)
    once1 = sweep_once(field, half, half, rows, cols)
    got_second, once1 = tied((got_second, once1))
    counts = second[2 * rows :] + got_second[2 * rows :]
    tiles, half0 = sweep_again_low(once0, rows, cols)
    face1, tiles = tied((face1, tiles))
    far = swapped(face1, "gy", lambda i: i ^ 1)
    lowered, half1 = sweep_again_high(once1, tiles)

    more = jnp.zeros_like(counts)
    mask = columns // 2
    while mask > 1:
        counts = counts + more
        more = swapped(counts, "gy", lambda i: i ^ mask)
        if mask == 4:
            more, half0 = tied((more, half0))
        if mask == 2:
            more, half1 = tied((more, half1))
        mask //= 2
    clow, chigh, counts = corners(got_first, got_second, counts, more)
    from_low = shifted(chigh, "gy", 1)
    from_high = shifted(clow, "gy", -1)
    lowered, edges = patch_z(got_first, got_second, half0, half1, lowered)
    total = distance.size * slabs * columns
    lowered = patch_near(edges, near, lowered)
    lowered, share = patch_far(
        100.0 / total, edges, near, far, from_low, from_high, counts, lowered
    )
    return (lowered, share[0, 0])


def solution(mesh):
    slabs, columns = mesh.shape["gz"], mesh.shape["gy"]
    if slabs != 4 or columns < 8 or columns & (columns - 1):
        raise ValueError("unsupported mesh")
    placed = (P("gz", "gy", None), P("gz", "gy", None), P(), P("gz", "gy", None))
    return jax.shard_map(
        on_device, mesh=mesh, in_specs=placed, out_specs=(P("gz", "gy", None), P()), check_vma=False
    )
```

profile of v0, /device:TPU:0, one launch (start us, length us, event | category | flops | bytes accessed | tf_op | source)
XLA Modules:
  0.0 41.6 jit_solution(774970612970469787)
XLA Ops:
  0.6 6.3 %raise_all.1 = (f32[66,200,128]{2,1,0:T(8,128)S(1)}, f32[40,1024]{1,0:T(8,128)S(1)}, f32[40,1024]{1,0:T(8,128)S(1)}) custom-call(f32[64,16,1024]{2,1,0:T(8,128)} %dist.1, s32[64,16,1024]{2,1,0:T(8,128)} %par.1, s32[32,128]{1,0:T(8,128)} %bitcast.2, s32[64,16,1024]{2,1,0:T(8,128)} %occ.1), custom_call_target="tpu_custom_call" | custom-call | bytes 12582912 | tf_op jit(solution)/shard_map/raise_all/pallas_call | solution.py:239
  6.9 2.5 %collective-permute-start = (f32[40,1024]{1,0:T(8,128)S(1)}, f32[40,1024]{1,0:T(8,128)S(1)}, u32[]{:S(2)}, u32[]{:S(2)}) collective-permute-start(f32[40,1024]{1,0:T(8,128)S(1)} %get-tuple-element.38), channel_id=1, source_target_pairs={{0,24},{8,16},{16,8},{24,0},{1,25},{9,17},{17,9},{25,1},{2,26},{10... | collective-permute-start | bytes 491528 | tf_op jit(solution)/shard_map/ppermute | solution.py:569
  9.4 0.8 %shard_map.62 = f32[2,64,1024]{2,1,0:T(8,128)S(1)} custom-call(f32[66,200,128]{2,1,0:T(8,128)S(1)} %get-tuple-element.39.field), custom_call_target="tpu_custom_call" | custom-call | bytes 2097152 | tf_op jit(solution)/shard_map/pallas_call | solution.py:136
  10.2 4.6 %collective-permute-start.4 = (f32[2,64,1024]{2,1,0:T(8,128)S(1)}, f32[2,64,1024]{2,1,0:T(8,128)S(1)}, u32[]{:S(2)}, u32[]{:S(2)}) collective-permute-start(f32[2,64,1024]{2,1,0:T(8,128)S(1)} %shard_map.62), channel_id=1, source_target_pairs={{0,7},{1,2},{2,1},{3,4},{4,3},{5,6},{6,5},{7,0},{8,15},{9,10},{10,... | collective-permute-start | bytes 1572872 | tf_op jit(solution)/shard_map/ppermute | solution.py:569
  14.8 0.8 %shard_map.61 = f32[2,64,1024]{2,1,0:T(8,128)S(1)} custom-call(f32[66,200,128]{2,1,0:T(8,128)S(1)} %get-tuple-element.39.field), custom_call_target="tpu_custom_call" | custom-call | bytes 2097152 | tf_op jit(solution)/shard_map/pallas_call | solution.py:136
  15.6 1.5 %shard_map.59.once = f32[34,200,128]{2,1,0:T(8,128)S(1)} custom-call(f32[66,200,128]{2,1,0:T(8,128)S(1)} %get-tuple-element.39.field), custom_call_target="tpu_custom_call" | custom-call | bytes 8388608 | tf_op jit(solution)/shard_map/pallas_call | solution.py:281
  17.2 0.0 collective-permute-done.first
  17.2 1.4 %sweep_again_low.1 = (f32[32,16,1024]{2,1,0:T(8,128)S(1)}, f32[4096,128]{1,0:T(8,128)S(1)}) custom-call(f32[34,200,128]{2,1,0:T(8,128)S(1)} %shard_map.59.once), custom_call_target="tpu_custom_call" | custom-call | bytes 8388608 | tf_op jit(solution)/shard_map/sweep_again_low/pallas_call | solution.py:333
  18.6 0.1 collective-permute-start.5
  18.7 0.5 %collective-permute-start.1 = (f32[40,1024]{1,0:T(8,128)S(1)}, f32[40,1024]{1,0:T(8,128)S(1)}, u32[]{:S(2)}, u32[]{:S(2)}) collective-permute-start(f32[40,1024]{1,0:T(8,128)S(1)} %fusion), channel_id=1, source_target_pairs={{0,8},{8,0},{16,24},{24,16},{1,9},{9,1},{17,25},{25,17},{2,10},{10... | collective-permute-start | bytes 491528 | tf_op jit(solution)/shard_map/ppermute | solution.py:569
  19.1 1.5 %shard_map.60.once = f32[34,200,128]{2,1,0:T(8,128)S(1)} custom-call(f32[66,200,128]{2,1,0:T(8,128)S(1)} %get-tuple-element.39.field), custom_call_target="tpu_custom_call" | custom-call | bytes 8388608 | tf_op jit(solution)/shard_map/pallas_call | solution.py:281
  20.6 0.0 collective-permute-done.1.second
  20.6 1.4 %collective-permute-start.2 = (f32[8,1024]{1,0:T(8,128)S(1)}, f32[8,1024]{1,0:T(8,128)S(1)}, u32[]{:S(2)}, u32[]{:S(2)}) collective-permute-start(f32[8,1024]{1,0:T(8,128)S(1)} %slice_add_fusion), channel_id=1, source_target_pairs={{0,4},{1,5},{2,6},{3,7},{4,0},{5,1},{6,2},{7,3},{8,12},{9,13},{10,... | collective-permute-start | bytes 98312 | tf_op jit(solution)/shard_map/ppermute | solution.py:569
  22.1 5.5 %collective-permute-done.2 = f32[8,1024]{1,0:T(8,128)S(1)} collective-permute-done((f32[8,1024]{1,0:T(8,128)S(1)}, f32[8,1024]{1,0:T(8,128)S(1)}, u32[]{:S(2)}, u32[]{:S(2)}) %collective-permute-start.2) | collective-permute-done | bytes 32800 | tf_op jit(solution)/shard_map/ppermute | solution.py:569
  27.6 2.2 %collective-permute-start.3 = (f32[8,1024]{1,0:T(8,128)S(1)}, f32[8,1024]{1,0:T(8,128)S(1)}, u32[]{:S(2)}, u32[]{:S(2)}) collective-permute-start(f32[8,1024]{1,0:T(8,128)S(1)} %add.15.counts), channel_id=1, source_target_pairs={{0,2},{1,3},{2,0},{3,1},{4,6},{5,7},{6,4},{7,5},{8,10},{9,11},{10,... | collective-permute-start | bytes 98312 | tf_op jit(solution)/shard_map/ppermute | solution.py:569
  29.7 2.0 %sweep_again_high.1 = (f32[64,16,1024]{2,1,0:T(8,128)}, f32[4096,128]{1,0:T(8,128)S(1)}) custom-call(f32[34,200,128]{2,1,0:T(8,128)S(1)} %shard_map.60.once, f32[32,16,1024]{2,1,0:T(8,128)S(1)} %get-tuple-element.49.low), custom_call_target="tpu_custom_call" | custom-call | bytes 8388608 | tf_op jit(solution)/shard_map/sweep_again_high/pallas_call | solution.py:350
  31.8 0.0 collective-permute-done.3.more
  31.8 1.7 %collective-permute-start.6 = (f32[8,1024]{1,0:T(8,128)S(1)}, f32[8,1024]{1,0:T(8,128)S(1)}, u32[]{:S(2)}, u32[]{:S(2)}) collective-permute-start(f32[8,1024]{1,0:T(8,128)S(1)} %get-tuple-element.56), channel_id=1, source_target_pairs={{0,1},{1,2},{2,3},{3,4},{4,5},{5,6},{6,7},{7,0},{8,9},{9,10},{10,1... | collective-permute-start | bytes 98312 | tf_op jit(solution)/shard_map/ppermute | solution.py:569
  33.5 3.1 %collective-permute-start.7 = (f32[8,1024]{1,0:T(8,128)S(1)}, f32[8,1024]{1,0:T(8,128)S(1)}, u32[]{:S(2)}, u32[]{:S(2)}) collective-permute-start(f32[8,1024]{1,0:T(8,128)S(1)} %get-tuple-element.57), channel_id=1, source_target_pairs={{0,7},{1,0},{2,1},{3,2},{4,3},{5,4},{6,5},{7,6},{8,15},{9,8},{10,9... | collective-permute-start | bytes 98312 | tf_op jit(solution)/shard_map/ppermute | solution.py:569
  36.6 0.8 %patch_z.1 = (f32[64,16,1024]{2,1,0:T(8,128)}, f32[4,64,1024]{2,1,0:T(8,128)S(1)}) custom-call(f32[40,1024]{1,0:T(8,128)S(1)} %collective-permute-done.first, f32[40,1024]{1,0:T(8,128)S(1)} %collective-permute-done.1.second, f32[4096,128]{1,0:T(8,128)S(1)} %get-tuple-element.45.slab_low, ...), custom_call_target="tpu_custom_call", output_to_operand_aliasing={{0}: (4, {})} | custom-call | bytes 1048576 | tf_op jit(solution)/shard_map/patch_z/pallas_call | solution.py:438
  37.4 0.0 collective-permute-done.4.near
  37.4 0.9 %patch_near.1._ = f32[64,16,1024]{2,1,0:T(8,128)} custom-call(f32[4,64,1024]{2,1,0:T(8,128)S(1)} %get-tuple-element.53.edges, f32[2,64,1024]{2,1,0:T(8,128)S(1)} %collective-permute-done.4.near, f32[64,16,1024]{2,1,0:T(8,128)} %get-tuple-element.59._), custom_call_target="tpu_custom_call", output_to_operand_aliasing={{}: (2, {})} | custom-call | bytes 1048576 | tf_op jit(solution)/shard_map/patch_near/pallas_call | solution.py:532
  38.2 0.4 collective-permute-done.6.clow
  38.6 1.6 %collective-permute-done.7.chigh = f32[8,1024]{1,0:T(8,128)S(1)} collective-permute-done((f32[8,1024]{1,0:T(8,128)S(1)}, f32[8,1024]{1,0:T(8,128)S(1)}, u32[]{:S(2)}, u32[]{:S(2)}) %collective-permute-start.7) | collective-permute-done | bytes 32800 | tf_op jit(solution)/shard_map/ppermute | solution.py:569
  40.2 0.0 collective-permute-done.5.far
  40.2 1.4 %patch_far.1 = (f32[64,16,1024]{2,1,0:T(8,128)}, f32[1,1]{1,0:T(1,128)}) custom-call(f32[4,64,1024]{2,1,0:T(8,128)S(1)} %get-tuple-element.53.edges, f32[2,64,1024]{2,1,0:T(8,128)S(1)} %collective-permute-done.4.near, f32[2,64,1024]{2,1,0:T(8,128)S(1)} %collective-permute-done.5.far, ...), custom_call_target="tpu_custom_call", output_to_operand_aliasing={{0}: (6, {})} | custom-call | bytes 1048576 | tf_op jit(solution)/shard_map/patch_far/pallas_call | solution.py:547
  (5 shorter events, 0.1 us)
Async XLA Ops:
  6.9 10.3 %collective-permute-start = (f32[40,1024]{1,0:T(8,128)S(1)}, f32[40,1024]{1,0:T(8,128)S(1)}, u32[]{:S(2)}, u32[]{:S(2)}) collective-permute-start(f32[40,1024]{1,0:T(8,128)S(1)} %get-tuple-element.38), channel_id=1, source_target_pairs={{0,24},{8,16},{16,8},{24,0},{1,25},{9,17},{17,9},{25,1},{2,26},{10... | collective-permute-start | bytes 491528 | tf_op jit(solution)/shard_map/ppermute | solution.py:569
  10.2 27.2 %collective-permute-start.4 = (f32[2,64,1024]{2,1,0:T(8,128)S(1)}, f32[2,64,1024]{2,1,0:T(8,128)S(1)}, u32[]{:S(2)}, u32[]{:S(2)}) collective-permute-start(f32[2,64,1024]{2,1,0:T(8,128)S(1)} %shard_map.62), channel_id=1, source_target_pairs={{0,7},{1,2},{2,1},{3,4},{4,3},{5,6},{6,5},{7,0},{8,15},{9,10},{10,... | collective-permute-start | bytes 1572872 | tf_op jit(solution)/shard_map/ppermute | solution.py:569
  18.6 21.6 %collective-permute-start.5 = (f32[2,64,1024]{2,1,0:T(8,128)S(1)}, f32[2,64,1024]{2,1,0:T(8,128)S(1)}, u32[]{:S(2)}, u32[]{:S(2)}) collective-permute-start(f32[2,64,1024]{2,1,0:T(8,128)S(1)} %shard_map.61), channel_id=1, source_target_pairs={{0,1},{1,0},{2,3},{3,2},{4,5},{5,4},{6,7},{7,6},{8,9},{9,8},{10,11... | collective-permute-start | bytes 1572872 | tf_op jit(solution)/shard_map/ppermute | solution.py:569
  18.7 2.0 %collective-permute-start.1 = (f32[40,1024]{1,0:T(8,128)S(1)}, f32[40,1024]{1,0:T(8,128)S(1)}, u32[]{:S(2)}, u32[]{:S(2)}) collective-permute-start(f32[40,1024]{1,0:T(8,128)S(1)} %fusion), channel_id=1, source_target_pairs={{0,8},{8,0},{16,24},{24,16},{1,9},{9,1},{17,25},{25,17},{2,10},{10... | collective-permute-start | bytes 491528 | tf_op jit(solution)/shard_map/ppermute | solution.py:569
  20.6 6.9 %collective-permute-start.2 = (f32[8,1024]{1,0:T(8,128)S(1)}, f32[8,1024]{1,0:T(8,128)S(1)}, u32[]{:S(2)}, u32[]{:S(2)}) collective-permute-start(f32[8,1024]{1,0:T(8,128)S(1)} %slice_add_fusion), channel_id=1, source_target_pairs={{0,4},{1,5},{2,6},{3,7},{4,0},{5,1},{6,2},{7,3},{8,12},{9,13},{10,... | collective-permute-start | bytes 98312 | tf_op jit(solution)/shard_map/ppermute | solution.py:569
  27.6 4.2 %collective-permute-start.3 = (f32[8,1024]{1,0:T(8,128)S(1)}, f32[8,1024]{1,0:T(8,128)S(1)}, u32[]{:S(2)}, u32[]{:S(2)}) collective-permute-start(f32[8,1024]{1,0:T(8,128)S(1)} %add.15.counts), channel_id=1, source_target_pairs={{0,2},{1,3},{2,0},{3,1},{4,6},{5,7},{6,4},{7,5},{8,10},{9,11},{10,... | collective-permute-start | bytes 98312 | tf_op jit(solution)/shard_map/ppermute | solution.py:569
  31.8 6.8 %collective-permute-start.6 = (f32[8,1024]{1,0:T(8,128)S(1)}, f32[8,1024]{1,0:T(8,128)S(1)}, u32[]{:S(2)}, u32[]{:S(2)}) collective-permute-start(f32[8,1024]{1,0:T(8,128)S(1)} %get-tuple-element.56), channel_id=1, source_target_pairs={{0,1},{1,2},{2,3},{3,4},{4,5},{5,6},{6,7},{7,0},{8,9},{9,10},{10,1... | collective-permute-start | bytes 98312 | tf_op jit(solution)/shard_map/ppermute | solution.py:569
  33.5 6.7 %collective-permute-start.7 = (f32[8,1024]{1,0:T(8,128)S(1)}, f32[8,1024]{1,0:T(8,128)S(1)}, u32[]{:S(2)}, u32[]{:S(2)}) collective-permute-start(f32[8,1024]{1,0:T(8,128)S(1)} %get-tuple-element.57), channel_id=1, source_target_pairs={{0,7},{1,0},{2,1},{3,2},{4,3},{5,4},{6,5},{7,6},{8,15},{9,8},{10,9... | collective-permute-start | bytes 98312 | tf_op jit(solution)/shard_map/ppermute | solution.py:569
where the time goes:
time: 41.8 us; the launch traced here: 41.6 us
  Pallas kernels  17.3 us (41%)
  starting transfers between devices  16 us (38%)
  waiting for transfers between devices  7.51 us (18%)
  between operations  0.78 us (2%)
    ppermute x8, starting transfers between devices, swapped(): lax.ppermute(value, axis, [(i, partner(i) % count) for i in range(count)])  16 us
    ppermute x8, waiting for transfers between devices, swapped(): lax.ppermute(value, axis, [(i, partner(i) % count) for i in range(count)])  7.51 us
    pallas_call x1, Pallas kernels, raise_all(): pl.pallas_call(raise_kernel, name='raise_all', out_shape=(jax.ShapeDtypeS...  6.25 us
    pallas_call x2, Pallas kernels, sweep_once(): pl.pallas_call(functools.partial(sweep_once_kernel, start, count, rows, c...  2.97 us
    pallas_call x1, Pallas kernels, sweep_again_high(): pl.pallas_call(sweep_again_high_kernel, name='sweep_again_high', out_shap...  2.04 us
    pallas_call x2, Pallas kernels, faces(): pl.pallas_call(functools.partial(faces_kernel, rows, cols, toward_odd), o...  1.63 us
    pallas_call x1, Pallas kernels, sweep_again_low(): pl.pallas_call(sweep_again_low_kernel, name='sweep_again_low', out_shape=...  1.4 us
    pallas_call x1, Pallas kernels, patch_far(): pl.pallas_call(functools.partial(patch_far_kernel, scale, lax.axis_size('...  1.4 us
  transfers between devices with their start and end apart: 8, of which 3 were waited for; matrix products, arithmetic and copies ran while one was open for 0% of the time, Pallas kernels for 23%

commit v1 on v0

--- a/solution.py
+++ b/solution.py
@@ -127,17 +127,21 @@
     lax.fori_loop(0, out.shape[1] // SUBLANES, body, 0)
 
 
-def faces_kernel(rows, cols, toward_odd, field, out):
+def faces_kernel(rows, cols, toward_odd, field, *outs):
     odd = lax.axis_index("gy") & 1
-    write_faces(field, rows, cols, odd == toward_odd, 0, out)
-
-
-def faces(field, rows, cols, toward_odd):
+    start = 0
+    for out in outs:
+        write_faces(field, rows, cols, odd == toward_odd, start, out)
+        start += out.shape[1]
+
+
+def faces(field, rows, cols, toward_odd, parts):
+    count = (field.shape[0] - 2) // parts
     return pl.pallas_call(
         functools.partial(faces_kernel, rows, cols, toward_odd),
-        out_shape=jax.ShapeDtypeStruct((2, field.shape[0] - 2, cols), jnp.float32),
+        out_shape=(jax.ShapeDtypeStruct((2, count, cols), jnp.float32),) * parts,
         in_specs=[VMEM],
-        out_specs=VMEM,
+        out_specs=(VMEM,) * parts,
         compiler_params=params(4),
         cost_estimate=cost(2),
     )(field)
@@ -454,11 +458,15 @@
     )(first, second, slab_low, slab_high, out)
 
 
-def merge_rows(away, edges, face, corner, missing, buf):
-    reach = face[1 - away] + VOXEL
-    if away:
-        reach = reach + VOXEL
-    buf[...] = jnp.minimum(edges[...], reach)
+def merge_rows(away, edges, parts, corner, missing, buf):
+    z = 0
+    for face in parts:
+        planes = pl.ds(z, face.shape[1])
+        reach = face[1 - away] + VOXEL
+        if away:
+            reach = reach + VOXEL
+        buf[planes, :] = jnp.minimum(edges[planes, :], reach)
+        z += face.shape[1]
     if corner is not None:
         for end, z in enumerate((0, buf.shape[0] - 1)):
             offer = jnp.where(missing[end], FAR, corner[pl.ds(end, 1), :])
@@ -470,15 +478,15 @@
     return (((0, 0), (1, 1)), ((rows - 1, 3), (rows - 2, 2)))
 
 
-def patch_near_kernel(edges, near, _, out, buf, sem):
+def patch_far_kernel(edges, far, _, out, buf, sem):
     odd = lax.axis_index("gy") & 1
     for side, places in enumerate(sides(out.shape[1])):
 
-        @pl.when(odd == side)
+        @pl.when(odd == 1 - side)
         def _():
             copies = []
             for away, (row, edge) in enumerate(places):
-                merge_rows(away, edges.at[edge], near, None, None, buf.at[away])
+                merge_rows(away, edges.at[edge], (far,), None, None, buf.at[away])
                 cp = pltpu.make_async_copy(buf.at[away], out.at[:, row, :], sem.at[away])
                 cp.start()
                 copies.append(cp)
@@ -486,8 +494,8 @@
                 cp.wait()
 
 
-def patch_far_kernel(
-    scale, slabs, edges, near, far, clow, chigh, counts, _, out, share, buf, lines, sem
+def patch_near_kernel(
+    scale, slabs, edges, near0, near1, far, clow, chigh, counts, _, out, share, buf, lines, sem
 ):
     depth, rows, _ = out.shape
     odd = lax.axis_index("gy") & 1
@@ -496,19 +504,19 @@
     corners = (clow, chigh)
     for side, places in enumerate(sides(rows)):
 
-        @pl.when(odd == 1 - side)
+        @pl.when(odd == side)
         def _():
             copies = []
             for away, (row, edge) in enumerate(places):
                 corner = None if away else corners[side]
-                merge_rows(away, edges.at[edge], far, corner, missing, buf.at[away])
+                merge_rows(away, edges.at[edge], (near0, near1), corner, missing, buf.at[away])
                 cp = pltpu.make_async_copy(buf.at[away], out.at[:, row, :], sem.at[away])
                 cp.start()
                 copies.append(cp)
             row, edge = sides(rows)[1 - side][0]
             for end, z in enumerate((0, depth - 1)):
                 line = pl.ds(z, 1)
-                reach = jnp.minimum(edges[edge, line, :], near[1, line, :] + VOXEL)
+                reach = jnp.minimum(edges[edge, line, :], far[1, line, :] + VOXEL)
                 offer = jnp.where(missing[end], FAR, corners[1 - side][pl.ds(end, 1), :])
                 lines[end] = jnp.minimum(reach, offer + VOXEL + VOXEL)
                 cp = pltpu.make_async_copy(
@@ -527,11 +535,11 @@
     share[...] = count[:, :1].astype(jnp.float32) * jnp.float32(scale)
 
 
-def patch_near(edges, near, out):
+def patch_far(edges, far, out):
     depth, _, cols = out.shape
     return pl.pallas_call(
-        patch_near_kernel,
-        name="patch_near",
+        patch_far_kernel,
+        name="patch_far",
         out_shape=jax.ShapeDtypeStruct(out.shape, out.dtype),
         in_specs=[VMEM] * 2 + [HBM],
         out_specs=HBM,
@@ -539,21 +547,21 @@
         scratch_shapes=[pltpu.VMEM((2, depth, cols), jnp.float32), pltpu.SemaphoreType.DMA((2,))],
         compiler_params=params(4),
         cost_estimate=cost(1),
-    )(edges, near, out)
-
-
-def patch_far(scale, edges, near, far, clow, chigh, counts, out):
+    )(edges, far, out)
+
+
+def patch_near(scale, edges, near0, near1, far, clow, chigh, counts, out):
     depth, _, cols = out.shape
     return pl.pallas_call(
-        functools.partial(patch_far_kernel, scale, lax.axis_size("gz")),
-        name="patch_far",
+        functools.partial(patch_near_kernel, scale, lax.axis_size("gz")),
+        name="patch_near",
         out_shape=(
             jax.ShapeDtypeStruct(out.shape, out.dtype),
             jax.ShapeDtypeStruct((1, 1), jnp.float32),
         ),
-        in_specs=[VMEM] * 6 + [HBM],
+        in_specs=[VMEM] * 7 + [HBM],
         out_specs=(HBM, VMEM),
-        input_output_aliases={6: 0},
+        input_output_aliases={7: 0},
         scratch_shapes=[
             pltpu.VMEM((2, depth, cols), jnp.float32),
             pltpu.VMEM((2, 1, cols), jnp.float32),
@@ -561,7 +569,7 @@
         ],
         compiler_params=params(4),
         cost_estimate=cost(1),
-    )(edges, near, far, clow, chigh, counts, out)
+    )(edges, near0, near1, far, clow, chigh, counts, out)
 
 
 def swapped(value, axis, partner):
@@ -587,11 +595,13 @@
         for a in (distance, parent, removed.reshape(-1, LANES), occupied)
     )
     field, first, second = raise_all(distance, parent, flags, occupied)
-    face0 = faces(field, rows, cols, 1)
-    near = swapped(face0, "gy", after_odd)
+    face0, face1 = faces(field, rows, cols, 1, 2)
+    near0 = swapped(face0, "gy", after_odd)
     got_first = swapped(first, "gz", after_odd)
-    face1 = faces(field, rows, cols, 0)
+    (face,) = faces(field, rows, cols, 0, 1)
     once0 = sweep_once(field, 0, half, rows, cols)
+    face, once0 = tied((face, once0))
+    far = swapped(face, "gy", lambda i: i ^ 1)
     got_first, once0 = tied((got_first, once0))
     second = second.at[2 * rows :].add(got_first[2 * rows :])
     got_second = swapped(second, "gz", lambda i: i ^ 1)
@@ -599,8 +609,6 @@
     got_second, once1 = tied((got_second, once1))
     counts = second[2 * rows :] + got_second[2 * rows :]
     tiles, half0 = sweep_again_low(once0, rows, cols)
-    face1, tiles = tied((face1, tiles))
-    far = swapped(face1, "gy", lambda i: i ^ 1)
     lowered, half1 = sweep_again_high(once1, tiles)
 
     more = jnp.zeros_like(counts)
@@ -611,16 +619,17 @@
         if mask == 4:
             more, half0 = tied((more, half0))
         if mask == 2:
-            more, half1 = tied((more, half1))
+            more, half1, face1 = tied((more, half1, face1))
         mask //= 2
+    near1 = swapped(face1, "gy", after_odd)
     clow, chigh, counts = corners(got_first, got_second, counts, more)
     from_low = shifted(chigh, "gy", 1)
     from_high = shifted(clow, "gy", -1)
     lowered, edges = patch_z(got_first, got_second, half0, half1, lowered)
     total = distance.size * slabs * columns
-    lowered = patch_near(edges, near, lowered)
-    lowered, share = patch_far(
-        100.0 / total, edges, near, far, from_low, from_high, counts, lowered
+    lowered = patch_far(edges, far, lowered)
+    lowered, share = patch_near(
+        100.0 / total, edges, near0, near1, far, from_low, from_high, counts, lowered
     )
     return (lowered, share[0, 0])
 

time: 41.8 us -> 43.7 us (1.045)
  starting transfers between devices: 16 us -> 18.5 us
  waiting for transfers between devices: 7.51 us -> 6.93 us
    ppermute x8 -> x9, starting transfers between devices: 16 us -> 18.5 us  [swapped(): lax.ppermute(value, axis, [(i, partner(i) % count) for i in range(count)])]
    ppermute x8 -> x9, waiting for transfers between devices: 7.51 us -> 6.93 us  [swapped(): lax.ppermute(value, axis, [(i, partner(i) % count) for i in range(count)])]
  transfers between devices with their start and end apart: 8 -> 9, of which waited for: 3 -> 5; matrix products, arithmetic and copies ran while one was open for 0% -> 0% of each run, Pallas kernels for 23% -> 22%
where the time goes in v1:
time: 43.7 us; the launch traced here: 43.5 us
  starting transfers between devices  18.5 us (42%)
  Pallas kernels  17.3 us (40%)
  waiting for transfers between devices  6.93 us (16%)
  between operations  0.76 us (2%)
    ppermute x9, starting transfers between devices, swapped(): lax.ppermute(value, axis, [(i, partner(i) % count) for i in range(count)])  18.5 us
    ppermute x9, waiting for transfers between devices, swapped(): lax.ppermute(value, axis, [(i, partner(i) % count) for i in range(count)])  6.93 us
    pallas_call x1, Pallas kernels, raise_all(): pl.pallas_call(raise_kernel, name='raise_all', out_shape=(jax.ShapeDtypeS...  6.25 us
    pallas_call x2, Pallas kernels, sweep_once(): pl.pallas_call(functools.partial(sweep_once_kernel, start, count, rows, c...  2.97 us
    pallas_call x1, Pallas kernels, sweep_again_high(): pl.pallas_call(sweep_again_high_kernel, name='sweep_again_high', out_shap...  2.04 us
    pallas_call x2, Pallas kernels, faces(): pl.pallas_call(functools.partial(faces_kernel, rows, cols, toward_odd), o...  1.62 us
    pallas_call x1, Pallas kernels, sweep_again_low(): pl.pallas_call(sweep_again_low_kernel, name='sweep_again_low', out_shape=...  1.39 us
    pallas_call x1, Pallas kernels, patch_near(): pl.pallas_call(functools.partial(patch_near_kernel, scale, lax.axis_size(...  1.39 us
  transfers between devices with their start and end apart: 9, of which 5 were waited for; matrix products, arithmetic and copies ran while one was open for 0% of the time, Pallas kernels for 22%

profile of v1, /device:TPU:0, one launch (start us, length us, event | category | flops | bytes accessed | tf_op | source)
XLA Modules:
  0.0 43.5 jit_solution(17067074291072471313)
XLA Ops:
  0.6 6.3 %raise_all.1 = (f32[66,200,128]{2,1,0:T(8,128)S(1)}, f32[40,1024]{1,0:T(8,128)S(1)}, f32[40,1024]{1,0:T(8,128)S(1)}) custom-call(f32[64,16,1024]{2,1,0:T(8,128)} %dist.1, s32[64,16,1024]{2,1,0:T(8,128)} %par.1, s32[32,128]{1,0:T(8,128)} %bitcast.2, s32[64,16,1024]{2,1,0:T(8,128)} %occ.1), custom_call_target="tpu_custom_call" | custom-call | bytes 12582912 | tf_op jit(solution)/shard_map/raise_all/pallas_call | solution.py:243
  6.9 2.5 %collective-permute-start = (f32[40,1024]{1,0:T(8,128)S(1)}, f32[40,1024]{1,0:T(8,128)S(1)}, u32[]{:S(2)}, u32[]{:S(2)}) collective-permute-start(f32[40,1024]{1,0:T(8,128)S(1)} %get-tuple-element.41), channel_id=1, source_target_pairs={{0,24},{8,16},{16,8},{24,0},{1,25},{9,17},{17,9},{25,1},{2,26},{10... | collective-permute-start | bytes 491528 | tf_op jit(solution)/shard_map/ppermute | solution.py:577
  9.4 0.8 %shard_map.59 = f32[2,64,1024]{2,1,0:T(8,128)S(1)} custom-call(f32[66,200,128]{2,1,0:T(8,128)S(1)} %get-tuple-element.42.field), custom_call_target="tpu_custom_call" | custom-call | bytes 2097152 | tf_op jit(solution)/shard_map/pallas_call | solution.py:140
  10.2 1.5 %shard_map.60.once = f32[34,200,128]{2,1,0:T(8,128)S(1)} custom-call(f32[66,200,128]{2,1,0:T(8,128)S(1)} %get-tuple-element.42.field), custom_call_target="tpu_custom_call" | custom-call | bytes 8388608 | tf_op jit(solution)/shard_map/pallas_call | solution.py:285
  11.7 2.3 %collective-permute-done.first = f32[40,1024]{1,0:T(8,128)S(1)} collective-permute-done((f32[40,1024]{1,0:T(8,128)S(1)}, f32[40,1024]{1,0:T(8,128)S(1)}, u32[]{:S(2)}, u32[]{:S(2)}) %collective-permute-start) | collective-permute-done | bytes 163872 | tf_op jit(solution)/shard_map/ppermute | solution.py:577
  14.0 0.1 collective-permute-start.1
  14.0 2.5 %collective-permute-start.6 = (f32[2,64,1024]{2,1,0:T(8,128)S(1)}, f32[2,64,1024]{2,1,0:T(8,128)S(1)}, u32[]{:S(2)}, u32[]{:S(2)}) collective-permute-start(f32[2,64,1024]{2,1,0:T(8,128)S(1)} %shard_map.59), channel_id=1, source_target_pairs={{0,1},{1,0},{2,3},{3,2},{4,5},{5,4},{6,7},{7,6},{8,9},{9,8},{10,11... | collective-permute-start | bytes 1572872 | tf_op jit(solution)/shard_map/ppermute | solution.py:577
  16.5 1.5 %shard_map.61.once = f32[34,200,128]{2,1,0:T(8,128)S(1)} custom-call(f32[66,200,128]{2,1,0:T(8,128)S(1)} %get-tuple-element.42.field), custom_call_target="tpu_custom_call" | custom-call | bytes 8388608 | tf_op jit(solution)/shard_map/pallas_call | solution.py:285
  18.0 0.0 collective-permute-done.1.second
  18.0 2.7 %collective-permute-start.2 = (f32[8,1024]{1,0:T(8,128)S(1)}, f32[8,1024]{1,0:T(8,128)S(1)}, u32[]{:S(2)}, u32[]{:S(2)}) collective-permute-start(f32[8,1024]{1,0:T(8,128)S(1)} %slice_add_fusion), channel_id=1, source_target_pairs={{0,4},{1,5},{2,6},{3,7},{4,0},{5,1},{6,2},{7,3},{8,12},{9,13},{10,... | collective-permute-start | bytes 98312 | tf_op jit(solution)/shard_map/ppermute | solution.py:577
  20.7 1.4 %sweep_again_low.1 = (f32[32,16,1024]{2,1,0:T(8,128)S(1)}, f32[4096,128]{1,0:T(8,128)S(1)}) custom-call(f32[34,200,128]{2,1,0:T(8,128)S(1)} %shard_map.60.once), custom_call_target="tpu_custom_call" | custom-call | bytes 8388608 | tf_op jit(solution)/shard_map/sweep_again_low/pallas_call | solution.py:337
  22.1 1.2 %collective-permute-done.2 = f32[8,1024]{1,0:T(8,128)S(1)} collective-permute-done((f32[8,1024]{1,0:T(8,128)S(1)}, f32[8,1024]{1,0:T(8,128)S(1)}, u32[]{:S(2)}, u32[]{:S(2)}) %collective-permute-start.2) | collective-permute-done | bytes 32800 | tf_op jit(solution)/shard_map/ppermute | solution.py:577
  23.3 1.2 %collective-permute-start.3 = (f32[8,1024]{1,0:T(8,128)S(1)}, f32[8,1024]{1,0:T(8,128)S(1)}, u32[]{:S(2)}, u32[]{:S(2)}) collective-permute-start(f32[8,1024]{1,0:T(8,128)S(1)} %add.15.counts), channel_id=1, source_target_pairs={{0,2},{1,3},{2,0},{3,1},{4,6},{5,7},{6,4},{7,5},{8,10},{9,11},{10,... | collective-permute-start | bytes 98312 | tf_op jit(solution)/shard_map/ppermute | solution.py:577
  24.5 0.8 %shard_map.62 = (f32[2,32,1024]{2,1,0:T(8,128)S(1)}, f32[2,32,1024]{2,1,0:T(8,128)S(1)}) custom-call(f32[66,200,128]{2,1,0:T(8,128)S(1)} %get-tuple-element.42.field), custom_call_target="tpu_custom_call" | custom-call | bytes 2097152 | tf_op jit(solution)/shard_map/pallas_call | solution.py:140
  25.3 2.5 %collective-permute-start.4 = (f32[2,32,1024]{2,1,0:T(8,128)S(1)}, f32[2,32,1024]{2,1,0:T(8,128)S(1)}, u32[]{:S(2)}, u32[]{:S(2)}) collective-permute-start(f32[2,32,1024]{2,1,0:T(8,128)S(1)} %get-tuple-element.58), channel_id=1, source_target_pairs={{0,7},{1,2},{2,1},{3,4},{4,3},{5,6},{6,5},{7,0},{8,15},{9,10},{10,... | collective-permute-start | bytes 786440 | tf_op jit(solution)/shard_map/ppermute | solution.py:577
  27.8 2.0 %sweep_again_high.1 = (f32[64,16,1024]{2,1,0:T(8,128)}, f32[4096,128]{1,0:T(8,128)S(1)}) custom-call(f32[34,200,128]{2,1,0:T(8,128)S(1)} %shard_map.61.once, f32[32,16,1024]{2,1,0:T(8,128)S(1)} %get-tuple-element.52.low), custom_call_target="tpu_custom_call" | custom-call | bytes 8388608 | tf_op jit(solution)/shard_map/sweep_again_high/pallas_call | solution.py:354
  29.9 0.0 collective-permute-done.3.more
  29.9 2.3 %collective-permute-start.5 = (f32[2,32,1024]{2,1,0:T(8,128)S(1)}, f32[2,32,1024]{2,1,0:T(8,128)S(1)}, u32[]{:S(2)}, u32[]{:S(2)}) collective-permute-start(f32[2,32,1024]{2,1,0:T(8,128)S(1)} %get-tuple-element.59), channel_id=1, source_target_pairs={{0,7},{1,2},{2,1},{3,4},{4,3},{5,6},{6,5},{7,0},{8,15},{9,10},{10,... | collective-permute-start | bytes 786440 | tf_op jit(solution)/shard_map/ppermute | solution.py:577
  32.2 0.1 collective-permute-start.7
  32.3 4.7 %collective-permute-start.8 = (f32[8,1024]{1,0:T(8,128)S(1)}, f32[8,1024]{1,0:T(8,128)S(1)}, u32[]{:S(2)}, u32[]{:S(2)}) collective-permute-start(f32[8,1024]{1,0:T(8,128)S(1)} %get-tuple-element.63), channel_id=1, source_target_pairs={{0,7},{1,0},{2,1},{3,2},{4,3},{5,4},{6,5},{7,6},{8,15},{9,8},{10,9... | collective-permute-start | bytes 98312 | tf_op jit(solution)/shard_map/ppermute | solution.py:577
  37.0 0.8 %patch_z.1 = (f32[64,16,1024]{2,1,0:T(8,128)}, f32[4,64,1024]{2,1,0:T(8,128)S(1)}) custom-call(f32[40,1024]{1,0:T(8,128)S(1)} %collective-permute-done.first, f32[40,1024]{1,0:T(8,128)S(1)} %collective-permute-done.1.second, f32[4096,128]{1,0:T(8,128)S(1)} %get-tuple-element.49.slab_low, ...), custom_call_target="tpu_custom_call", output_to_operand_aliasing={{0}: (4, {})} | custom-call | bytes 1048576 | tf_op jit(solution)/shard_map/patch_z/pallas_call | solution.py:442
  37.8 2.8 %collective-permute-done.6.far = f32[2,64,1024]{2,1,0:T(8,128)S(1)} collective-permute-done((f32[2,64,1024]{2,1,0:T(8,128)S(1)}, f32[2,64,1024]{2,1,0:T(8,128)S(1)}, u32[]{:S(2)}, u32[]{:S(2)}) %collective-permute-start.6) | collective-permute-done | bytes 524320 | tf_op jit(solution)/shard_map/ppermute | solution.py:577
  40.6 0.8 %patch_far.1._ = f32[64,16,1024]{2,1,0:T(8,128)} custom-call(f32[4,64,1024]{2,1,0:T(8,128)S(1)} %get-tuple-element.57.edges, f32[2,64,1024]{2,1,0:T(8,128)S(1)} %collective-permute-done.6.far, f32[64,16,1024]{2,1,0:T(8,128)} %get-tuple-element.65._), custom_call_target="tpu_custom_call", output_to_operand_aliasing={{}: (2, {})} | custom-call | bytes 1048576 | tf_op jit(solution)/shard_map/patch_far/pallas_call | solution.py:540
  41.4 0.0 collective-permute-done.4.near0
  41.4 0.1 collective-permute-done.7.clow
  41.5 0.6 %collective-permute-done.8.chigh = f32[8,1024]{1,0:T(8,128)S(1)} collective-permute-done((f32[8,1024]{1,0:T(8,128)S(1)}, f32[8,1024]{1,0:T(8,128)S(1)}, u32[]{:S(2)}, u32[]{:S(2)}) %collective-permute-start.8) | collective-permute-done | bytes 32800 | tf_op jit(solution)/shard_map/ppermute | solution.py:577
  42.1 0.0 collective-permute-done.5.near1
  42.1 1.4 %patch_near.1 = (f32[64,16,1024]{2,1,0:T(8,128)}, f32[1,1]{1,0:T(1,128)}) custom-call(f32[4,64,1024]{2,1,0:T(8,128)S(1)} %get-tuple-element.57.edges, f32[2,32,1024]{2,1,0:T(8,128)S(1)} %collective-permute-done.4.near0, f32[2,32,1024]{2,1,0:T(8,128)S(1)} %collective-permute-done.5.near1, ...), custom_call_target="tpu_custom_call", output_to_operand_aliasing={{0}: (7, {})} | custom-call | bytes 1048576 | tf_op jit(solution)/shard_map/patch_near/pallas_call | solution.py:555
  (5 shorter events, 0.0 us)
Async XLA Ops:
  6.9 7.1 %collective-permute-start = (f32[40,1024]{1,0:T(8,128)S(1)}, f32[40,1024]{1,0:T(8,128)S(1)}, u32[]{:S(2)}, u32[]{:S(2)}) collective-permute-start(f32[40,1024]{1,0:T(8,128)S(1)} %get-tuple-element.41), channel_id=1, source_target_pairs={{0,24},{8,16},{16,8},{24,0},{1,25},{9,17},{17,9},{25,1},{2,26},{10... | collective-permute-start | bytes 491528 | tf_op jit(solution)/shard_map/ppermute | solution.py:577
  14.0 4.1 %collective-permute-start.1 = (f32[40,1024]{1,0:T(8,128)S(1)}, f32[40,1024]{1,0:T(8,128)S(1)}, u32[]{:S(2)}, u32[]{:S(2)}) collective-permute-start(f32[40,1024]{1,0:T(8,128)S(1)} %fusion), channel_id=1, source_target_pairs={{0,8},{8,0},{16,24},{24,16},{1,9},{9,1},{17,25},{25,17},{2,10},{10... | collective-permute-start | bytes 491528 | tf_op jit(solution)/shard_map/ppermute | solution.py:577
  14.0 26.5 %collective-permute-start.6 = (f32[2,64,1024]{2,1,0:T(8,128)S(1)}, f32[2,64,1024]{2,1,0:T(8,128)S(1)}, u32[]{:S(2)}, u32[]{:S(2)}) collective-permute-start(f32[2,64,1024]{2,1,0:T(8,128)S(1)} %shard_map.59), channel_id=1, source_target_pairs={{0,1},{1,0},{2,3},{3,2},{4,5},{5,4},{6,7},{7,6},{8,9},{9,8},{10,11... | collective-permute-start | bytes 1572872 | tf_op jit(solution)/shard_map/ppermute | solution.py:577
  18.0 5.2 %collective-permute-start.2 = (f32[8,1024]{1,0:T(8,128)S(1)}, f32[8,1024]{1,0:T(8,128)S(1)}, u32[]{:S(2)}, u32[]{:S(2)}) collective-permute-start(f32[8,1024]{1,0:T(8,128)S(1)} %slice_add_fusion), channel_id=1, source_target_pairs={{0,4},{1,5},{2,6},{3,7},{4,0},{5,1},{6,2},{7,3},{8,12},{9,13},{10,... | collective-permute-start | bytes 98312 | tf_op jit(solution)/shard_map/ppermute | solution.py:577
  23.3 6.6 %collective-permute-start.3 = (f32[8,1024]{1,0:T(8,128)S(1)}, f32[8,1024]{1,0:T(8,128)S(1)}, u32[]{:S(2)}, u32[]{:S(2)}) collective-permute-start(f32[8,1024]{1,0:T(8,128)S(1)} %add.15.counts), channel_id=1, source_target_pairs={{0,2},{1,3},{2,0},{3,1},{4,6},{5,7},{6,4},{7,5},{8,10},{9,11},{10,... | collective-permute-start | bytes 98312 | tf_op jit(solution)/shard_map/ppermute | solution.py:577
  25.3 16.1 %collective-permute-start.4 = (f32[2,32,1024]{2,1,0:T(8,128)S(1)}, f32[2,32,1024]{2,1,0:T(8,128)S(1)}, u32[]{:S(2)}, u32[]{:S(2)}) collective-permute-start(f32[2,32,1024]{2,1,0:T(8,128)S(1)} %get-tuple-element.58), channel_id=1, source_target_pairs={{0,7},{1,2},{2,1},{3,4},{4,3},{5,6},{6,5},{7,0},{8,15},{9,10},{10,... | collective-permute-start | bytes 786440 | tf_op jit(solution)/shard_map/ppermute | solution.py:577
  29.9 12.3 %collective-permute-start.5 = (f32[2,32,1024]{2,1,0:T(8,128)S(1)}, f32[2,32,1024]{2,1,0:T(8,128)S(1)}, u32[]{:S(2)}, u32[]{:S(2)}) collective-permute-start(f32[2,32,1024]{2,1,0:T(8,128)S(1)} %get-tuple-element.59), channel_id=1, source_target_pairs={{0,7},{1,2},{2,1},{3,4},{4,3},{5,6},{6,5},{7,0},{8,15},{9,10},{10,... | collective-permute-start | bytes 786440 | tf_op jit(solution)/shard_map/ppermute | solution.py:577
  32.2 9.3 %collective-permute-start.7 = (f32[8,1024]{1,0:T(8,128)S(1)}, f32[8,1024]{1,0:T(8,128)S(1)}, u32[]{:S(2)}, u32[]{:S(2)}) collective-permute-start(f32[8,1024]{1,0:T(8,128)S(1)} %get-tuple-element.62), channel_id=1, source_target_pairs={{0,1},{1,2},{2,3},{3,4},{4,5},{5,6},{6,7},{7,0},{8,9},{9,10},{10,1... | collective-permute-start | bytes 98312 | tf_op jit(solution)/shard_map/ppermute | solution.py:577
  32.3 9.8 %collective-permute-start.8 = (f32[8,1024]{1,0:T(8,128)S(1)}, f32[8,1024]{1,0:T(8,128)S(1)}, u32[]{:S(2)}, u32[]{:S(2)}) collective-permute-start(f32[8,1024]{1,0:T(8,128)S(1)} %get-tuple-element.63), channel_id=1, source_target_pairs={{0,7},{1,0},{2,1},{3,2},{4,3},{5,4},{6,5},{7,6},{8,15},{9,8},{10,9... | collective-permute-start | bytes 98312 | tf_op jit(solution)/shard_map/ppermute | solution.py:577

commit v2 on v1

--- a/solution.py
+++ b/solution.py
@@ -135,13 +135,12 @@
         start += out.shape[1]
 
 
-def faces(field, rows, cols, toward_odd, parts):
-    count = (field.shape[0] - 2) // parts
+def faces(field, rows, cols, toward_odd, counts):
     return pl.pallas_call(
         functools.partial(faces_kernel, rows, cols, toward_odd),
-        out_shape=(jax.ShapeDtypeStruct((2, count, cols), jnp.float32),) * parts,
+        out_shape=tuple(jax.ShapeDtypeStruct((2, n, cols), jnp.float32) for n in counts),
         in_specs=[VMEM],
-        out_specs=(VMEM,) * parts,
+        out_specs=(VMEM,) * len(counts),
         compiler_params=params(4),
         cost_estimate=cost(2),
     )(field)
@@ -588,6 +587,7 @@
 def on_device(distance, parent, removed, occupied):
     depth, rows, cols = distance.shape
     half = depth // 2
+    most = depth // 4 * 3
     slabs, columns = lax.axis_size("gz"), lax.axis_size("gy")
     tied = lax.optimization_barrier
     distance, parent, flags, occupied = (
@@ -595,10 +595,10 @@
         for a in (distance, parent, removed.reshape(-1, LANES), occupied)
     )
     field, first, second = raise_all(distance, parent, flags, occupied)
-    face0, face1 = faces(field, rows, cols, 1, 2)
+    face0, face1 = faces(field, rows, cols, 1, (most, depth - most))
     near0 = swapped(face0, "gy", after_odd)
     got_first = swapped(first, "gz", after_odd)
-    (face,) = faces(field, rows, cols, 0, 1)
+    (face,) = faces(field, rows, cols, 0, (depth,))
     once0 = sweep_once(field, 0, half, rows, cols)
     face, once0 = tied((face, once0))
     far = swapped(face, "gy", lambda i: i ^ 1)

time: 43.7 us -> 46.5 us (1.064)
  waiting for transfers between devices: 6.93 us -> 9.14 us
  starting transfers between devices: 18.5 us -> 19.1 us
    ppermute x9, waiting for transfers between devices: 6.93 us -> 9.14 us  [swapped(): lax.ppermute(value, axis, [(i, partner(i) % count) for i in range(count)])]
    ppermute x9, starting transfers between devices: 18.5 us -> 19.1 us  [swapped(): lax.ppermute(value, axis, [(i, partner(i) % count) for i in range(count)])]
  transfers between devices with their start and end apart: 9 -> 9, of which waited for: 5 -> 3; matrix products, arithmetic and copies ran while one was open for 0% -> 0% of each run, Pallas kernels for 22% -> 21%
where the time goes in v2:
time: 46.5 us; the launch traced here: 46.4 us
  starting transfers between devices  19.1 us (41%)
  Pallas kernels  17.3 us (37%)
  waiting for transfers between devices  9.14 us (20%)
  between operations  0.78 us (2%)
    ppermute x9, starting transfers between devices, swapped(): lax.ppermute(value, axis, [(i, partner(i) % count) for i in range(count)])  19.1 us
    ppermute x9, waiting for transfers between devices, swapped(): lax.ppermute(value, axis, [(i, partner(i) % count) for i in range(count)])  9.14 us
    pallas_call x1, Pallas kernels, raise_all(): pl.pallas_call(raise_kernel, name='raise_all', out_shape=(jax.ShapeDtypeS...  6.25 us
    pallas_call x2, Pallas kernels, sweep_once(): pl.pallas_call(functools.partial(sweep_once_kernel, start, count, rows, c...  2.97 us
    pallas_call x1, Pallas kernels, sweep_again_high(): pl.pallas_call(sweep_again_high_kernel, name='sweep_again_high', out_shap...  2.04 us
    pallas_call x2, Pallas kernels, faces(): pl.pallas_call(functools.partial(faces_kernel, rows, cols, toward_odd), o...  1.62 us
    pallas_call x1, Pallas kernels, sweep_again_low(): pl.pallas_call(sweep_again_low_kernel, name='sweep_again_low', out_shape=...  1.4 us
    pallas_call x1, Pallas kernels, patch_near(): pl.pallas_call(functools.partial(patch_near_kernel, scale, lax.axis_size(...  1.39 us
  transfers between devices with their start and end apart: 9, of which 3 were waited for; matrix products, arithmetic and copies ran while one was open for 0% of the time, Pallas kernels for 21%

profile of v2, /device:TPU:0, one launch (start us, length us, event | category | flops | bytes accessed | tf_op | source)
XLA Modules:
  0.0 46.4 jit_solution(102498904276509259)
XLA Ops:
  0.6 6.3 %raise_all.1 = (f32[66,200,128]{2,1,0:T(8,128)S(1)}, f32[40,1024]{1,0:T(8,128)S(1)}, f32[40,1024]{1,0:T(8,128)S(1)}) custom-call(f32[64,16,1024]{2,1,0:T(8,128)} %dist.1, s32[64,16,1024]{2,1,0:T(8,128)} %par.1, s32[32,128]{1,0:T(8,128)} %bitcast.2, s32[64,16,1024]{2,1,0:T(8,128)} %occ.1), custom_call_target="tpu_custom_call" | custom-call | bytes 12582912 | tf_op jit(solution)/shard_map/raise_all/pallas_call | solution.py:242
  6.9 2.5 %collective-permute-start = (f32[40,1024]{1,0:T(8,128)S(1)}, f32[40,1024]{1,0:T(8,128)S(1)}, u32[]{:S(2)}, u32[]{:S(2)}) collective-permute-start(f32[40,1024]{1,0:T(8,128)S(1)} %get-tuple-element.41), channel_id=1, source_target_pairs={{0,24},{8,16},{16,8},{24,0},{1,25},{9,17},{17,9},{25,1},{2,26},{10... | collective-permute-start | bytes 491528 | tf_op jit(solution)/shard_map/ppermute | solution.py:576
  9.4 0.8 %shard_map.59 = f32[2,64,1024]{2,1,0:T(8,128)S(1)} custom-call(f32[66,200,128]{2,1,0:T(8,128)S(1)} %get-tuple-element.42.field), custom_call_target="tpu_custom_call" | custom-call | bytes 2097152 | tf_op jit(solution)/shard_map/pallas_call | solution.py:139
  10.2 1.5 %shard_map.60.once = f32[34,200,128]{2,1,0:T(8,128)S(1)} custom-call(f32[66,200,128]{2,1,0:T(8,128)S(1)} %get-tuple-element.42.field), custom_call_target="tpu_custom_call" | custom-call | bytes 8388608 | tf_op jit(solution)/shard_map/pallas_call | solution.py:284
  11.7 2.2 %collective-permute-done.first = f32[40,1024]{1,0:T(8,128)S(1)} collective-permute-done((f32[40,1024]{1,0:T(8,128)S(1)}, f32[40,1024]{1,0:T(8,128)S(1)}, u32[]{:S(2)}, u32[]{:S(2)}) %collective-permute-start) | collective-permute-done | bytes 163872 | tf_op jit(solution)/shard_map/ppermute | solution.py:576
  14.0 0.1 collective-permute-start.1
  14.0 2.5 %collective-permute-start.6 = (f32[2,64,1024]{2,1,0:T(8,128)S(1)}, f32[2,64,1024]{2,1,0:T(8,128)S(1)}, u32[]{:S(2)}, u32[]{:S(2)}) collective-permute-start(f32[2,64,1024]{2,1,0:T(8,128)S(1)} %shard_map.59), channel_id=1, source_target_pairs={{0,1},{1,0},{2,3},{3,2},{4,5},{5,4},{6,7},{7,6},{8,9},{9,8},{10,11... | collective-permute-start | bytes 1572872 | tf_op jit(solution)/shard_map/ppermute | solution.py:576
  16.5 0.8 %shard_map.62 = (f32[2,48,1024]{2,1,0:T(8,128)S(1)}, f32[2,16,1024]{2,1,0:T(8,128)S(1)}) custom-call(f32[66,200,128]{2,1,0:T(8,128)S(1)} %get-tuple-element.42.field), custom_call_target="tpu_custom_call" | custom-call | bytes 2097152 | tf_op jit(solution)/shard_map/pallas_call | solution.py:139
  17.3 3.6 %collective-permute-start.4 = (f32[2,48,1024]{2,1,0:T(8,128)S(1)}, f32[2,48,1024]{2,1,0:T(8,128)S(1)}, u32[]{:S(2)}, u32[]{:S(2)}) collective-permute-start(f32[2,48,1024]{2,1,0:T(8,128)S(1)} %get-tuple-element.58), channel_id=1, source_target_pairs={{0,7},{1,2},{2,1},{3,4},{4,3},{5,6},{6,5},{7,0},{8,15},{9,10},{10,... | collective-permute-start | bytes 1179656 | tf_op jit(solution)/shard_map/ppermute | solution.py:576
  21.0 1.5 %shard_map.61.once = f32[34,200,128]{2,1,0:T(8,128)S(1)} custom-call(f32[66,200,128]{2,1,0:T(8,128)S(1)} %get-tuple-element.42.field), custom_call_target="tpu_custom_call" | custom-call | bytes 8388608 | tf_op jit(solution)/shard_map/pallas_call | solution.py:284
  22.4 0.0 collective-permute-done.1.second
  22.5 0.1 collective-permute-start.2
  22.6 1.4 %sweep_again_low.1 = (f32[32,16,1024]{2,1,0:T(8,128)S(1)}, f32[4096,128]{1,0:T(8,128)S(1)}) custom-call(f32[34,200,128]{2,1,0:T(8,128)S(1)} %shard_map.60.once), custom_call_target="tpu_custom_call" | custom-call | bytes 8388608 | tf_op jit(solution)/shard_map/sweep_again_low/pallas_call | solution.py:336
  24.0 6.6 %collective-permute-done.2 = f32[8,1024]{1,0:T(8,128)S(1)} collective-permute-done((f32[8,1024]{1,0:T(8,128)S(1)}, f32[8,1024]{1,0:T(8,128)S(1)}, u32[]{:S(2)}, u32[]{:S(2)}) %collective-permute-start.2) | collective-permute-done | bytes 32800 | tf_op jit(solution)/shard_map/ppermute | solution.py:576
  30.6 1.9 %collective-permute-start.3 = (f32[8,1024]{1,0:T(8,128)S(1)}, f32[8,1024]{1,0:T(8,128)S(1)}, u32[]{:S(2)}, u32[]{:S(2)}) collective-permute-start(f32[8,1024]{1,0:T(8,128)S(1)} %add.15.counts), channel_id=1, source_target_pairs={{0,2},{1,3},{2,0},{3,1},{4,6},{5,7},{6,4},{7,5},{8,10},{9,11},{10,... | collective-permute-start | bytes 98312 | tf_op jit(solution)/shard_map/ppermute | solution.py:576
  32.5 2.0 %sweep_again_high.1 = (f32[64,16,1024]{2,1,0:T(8,128)}, f32[4096,128]{1,0:T(8,128)S(1)}) custom-call(f32[34,200,128]{2,1,0:T(8,128)S(1)} %shard_map.61.once, f32[32,16,1024]{2,1,0:T(8,128)S(1)} %get-tuple-element.52.low), custom_call_target="tpu_custom_call" | custom-call | bytes 8388608 | tf_op jit(solution)/shard_map/sweep_again_high/pallas_call | solution.py:353
  34.6 0.0 collective-permute-done.3.more
  34.6 3.7 %collective-permute-start.5 = (f32[2,16,1024]{2,1,0:T(8,128)S(1)}, f32[2,16,1024]{2,1,0:T(8,128)S(1)}, u32[]{:S(2)}, u32[]{:S(2)}) collective-permute-start(f32[2,16,1024]{2,1,0:T(8,128)S(1)} %get-tuple-element.59), channel_id=1, source_target_pairs={{0,7},{1,2},{2,1},{3,4},{4,3},{5,6},{6,5},{7,0},{8,15},{9,10},{10,... | collective-permute-start | bytes 393224 | tf_op jit(solution)/shard_map/ppermute | solution.py:576
  38.3 0.1 collective-permute-start.7
  38.4 4.7 %collective-permute-start.8 = (f32[8,1024]{1,0:T(8,128)S(1)}, f32[8,1024]{1,0:T(8,128)S(1)}, u32[]{:S(2)}, u32[]{:S(2)}) collective-permute-start(f32[8,1024]{1,0:T(8,128)S(1)} %get-tuple-element.63), channel_id=1, source_target_pairs={{0,7},{1,0},{2,1},{3,2},{4,3},{5,4},{6,5},{7,6},{8,15},{9,8},{10,9... | collective-permute-start | bytes 98312 | tf_op jit(solution)/shard_map/ppermute | solution.py:576
  43.1 0.8 %patch_z.1 = (f32[64,16,1024]{2,1,0:T(8,128)}, f32[4,64,1024]{2,1,0:T(8,128)S(1)}) custom-call(f32[40,1024]{1,0:T(8,128)S(1)} %collective-permute-done.first, f32[40,1024]{1,0:T(8,128)S(1)} %collective-permute-done.1.second, f32[4096,128]{1,0:T(8,128)S(1)} %get-tuple-element.49.slab_low, ...), custom_call_target="tpu_custom_call", output_to_operand_aliasing={{0}: (4, {})} | custom-call | bytes 1048576 | tf_op jit(solution)/shard_map/patch_z/pallas_call | solution.py:441
  43.9 0.0 collective-permute-done.6.far
  43.9 0.9 %patch_far.1._ = f32[64,16,1024]{2,1,0:T(8,128)} custom-call(f32[4,64,1024]{2,1,0:T(8,128)S(1)} %get-tuple-element.57.edges, f32[2,64,1024]{2,1,0:T(8,128)S(1)} %collective-permute-done.6.far, f32[64,16,1024]{2,1,0:T(8,128)} %get-tuple-element.65._), custom_call_target="tpu_custom_call", output_to_operand_aliasing={{}: (2, {})} | custom-call | bytes 1048576 | tf_op jit(solution)/shard_map/patch_far/pallas_call | solution.py:539
  44.7 0.0 collective-permute-done.4.near0
  44.7 0.2 collective-permute-done.7.clow
  45.0 0.0 collective-permute-done.8.chigh
  45.0 0.0 collective-permute-done.5.near1
  45.0 1.4 %patch_near.1 = (f32[64,16,1024]{2,1,0:T(8,128)}, f32[1,1]{1,0:T(1,128)}) custom-call(f32[4,64,1024]{2,1,0:T(8,128)S(1)} %get-tuple-element.57.edges, f32[2,48,1024]{2,1,0:T(8,128)S(1)} %collective-permute-done.4.near0, f32[2,16,1024]{2,1,0:T(8,128)S(1)} %collective-permute-done.5.near1, ...), custom_call_target="tpu_custom_call", output_to_operand_aliasing={{0}: (7, {})} | custom-call | bytes 1048576 | tf_op jit(solution)/shard_map/patch_near/pallas_call | solution.py:554
  (5 shorter events, 0.0 us)
Async XLA Ops:
  6.9 7.1 %collective-permute-start = (f32[40,1024]{1,0:T(8,128)S(1)}, f32[40,1024]{1,0:T(8,128)S(1)}, u32[]{:S(2)}, u32[]{:S(2)}) collective-permute-start(f32[40,1024]{1,0:T(8,128)S(1)} %get-tuple-element.41), channel_id=1, source_target_pairs={{0,24},{8,16},{16,8},{24,0},{1,25},{9,17},{17,9},{25,1},{2,26},{10... | collective-permute-start | bytes 491528 | tf_op jit(solution)/shard_map/ppermute | solution.py:576
  14.0 8.5 %collective-permute-start.1 = (f32[40,1024]{1,0:T(8,128)S(1)}, f32[40,1024]{1,0:T(8,128)S(1)}, u32[]{:S(2)}, u32[]{:S(2)}) collective-permute-start(f32[40,1024]{1,0:T(8,128)S(1)} %fusion), channel_id=1, source_target_pairs={{0,8},{8,0},{16,24},{24,16},{1,9},{9,1},{17,25},{25,17},{2,10},{10... | collective-permute-start | bytes 491528 | tf_op jit(solution)/shard_map/ppermute | solution.py:576
  14.0 29.8 %collective-permute-start.6 = (f32[2,64,1024]{2,1,0:T(8,128)S(1)}, f32[2,64,1024]{2,1,0:T(8,128)S(1)}, u32[]{:S(2)}, u32[]{:S(2)}) collective-permute-start(f32[2,64,1024]{2,1,0:T(8,128)S(1)} %shard_map.59), channel_id=1, source_target_pairs={{0,1},{1,0},{2,3},{3,2},{4,5},{5,4},{6,7},{7,6},{8,9},{9,8},{10,11... | collective-permute-start | bytes 1572872 | tf_op jit(solution)/shard_map/ppermute | solution.py:576
  17.3 27.4 %collective-permute-start.4 = (f32[2,48,1024]{2,1,0:T(8,128)S(1)}, f32[2,48,1024]{2,1,0:T(8,128)S(1)}, u32[]{:S(2)}, u32[]{:S(2)}) collective-permute-start(f32[2,48,1024]{2,1,0:T(8,128)S(1)} %get-tuple-element.58), channel_id=1, source_target_pairs={{0,7},{1,2},{2,1},{3,4},{4,3},{5,6},{6,5},{7,0},{8,15},{9,10},{10,... | collective-permute-start | bytes 1179656 | tf_op jit(solution)/shard_map/ppermute | solution.py:576
  22.5 8.1 %collective-permute-start.2 = (f32[8,1024]{1,0:T(8,128)S(1)}, f32[8,1024]{1,0:T(8,128)S(1)}, u32[]{:S(2)}, u32[]{:S(2)}) collective-permute-start(f32[8,1024]{1,0:T(8,128)S(1)} %slice_add_fusion), channel_id=1, source_target_pairs={{0,4},{1,5},{2,6},{3,7},{4,0},{5,1},{6,2},{7,3},{8,12},{9,13},{10,... | collective-permute-start | bytes 98312 | tf_op jit(solution)/shard_map/ppermute | solution.py:576
  30.6 4.0 %collective-permute-start.3 = (f32[8,1024]{1,0:T(8,128)S(1)}, f32[8,1024]{1,0:T(8,128)S(1)}, u32[]{:S(2)}, u32[]{:S(2)}) collective-permute-start(f32[8,1024]{1,0:T(8,128)S(1)} %add.15.counts), channel_id=1, source_target_pairs={{0,2},{1,3},{2,0},{3,1},{4,6},{5,7},{6,4},{7,5},{8,10},{9,11},{10,... | collective-permute-start | bytes 98312 | tf_op jit(solution)/shard_map/ppermute | solution.py:576
  34.6 10.4 %collective-permute-start.5 = (f32[2,16,1024]{2,1,0:T(8,128)S(1)}, f32[2,16,1024]{2,1,0:T(8,128)S(1)}, u32[]{:S(2)}, u32[]{:S(2)}) collective-permute-start(f32[2,16,1024]{2,1,0:T(8,128)S(1)} %get-tuple-element.59), channel_id=1, source_target_pairs={{0,7},{1,2},{2,1},{3,4},{4,3},{5,6},{6,5},{7,0},{8,15},{9,10},{10,... | collective-permute-start | bytes 393224 | tf_op jit(solution)/shard_map/ppermute | solution.py:576
  38.3 6.7 %collective-permute-start.7 = (f32[8,1024]{1,0:T(8,128)S(1)}, f32[8,1024]{1,0:T(8,128)S(1)}, u32[]{:S(2)}, u32[]{:S(2)}) collective-permute-start(f32[8,1024]{1,0:T(8,128)S(1)} %get-tuple-element.62), channel_id=1, source_target_pairs={{0,1},{1,2},{2,3},{3,4},{4,5},{5,6},{6,7},{7,0},{8,9},{9,10},{10,1... | collective-permute-start | bytes 98312 | tf_op jit(solution)/shard_map/ppermute | solution.py:576
  38.4 6.6 %collective-permute-start.8 = (f32[8,1024]{1,0:T(8,128)S(1)}, f32[8,1024]{1,0:T(8,128)S(1)}, u32[]{:S(2)}, u32[]{:S(2)}) collective-permute-start(f32[8,1024]{1,0:T(8,128)S(1)} %get-tuple-element.63), channel_id=1, source_target_pairs={{0,7},{1,0},{2,1},{3,2},{4,3},{5,4},{6,5},{7,6},{8,15},{9,8},{10,9... | collective-permute-start | bytes 98312 | tf_op jit(solution)/shard_map/ppermute | solution.py:576

commit v3 on v0

--- a/solution.py
+++ b/solution.py
@@ -474,7 +474,7 @@
     odd = lax.axis_index("gy") & 1
     for side, places in enumerate(sides(out.shape[1])):
 
-        @pl.when(odd == side)
+        @pl.when(odd == 1 - side)
         def _():
             copies = []
             for away, (row, edge) in enumerate(places):
@@ -496,7 +496,7 @@
     corners = (clow, chigh)
     for side, places in enumerate(sides(rows)):
 
-        @pl.when(odd == 1 - side)
+        @pl.when(odd == side)
         def _():
             copies = []
             for away, (row, edge) in enumerate(places):
@@ -587,32 +587,35 @@
         for a in (distance, parent, removed.reshape(-1, LANES), occupied)
     )
     field, first, second = raise_all(distance, parent, flags, occupied)
-    face0 = faces(field, rows, cols, 1)
-    near = swapped(face0, "gy", after_odd)
-    got_first = swapped(first, "gz", after_odd)
-    face1 = faces(field, rows, cols, 0)
+    face0 = faces(field, rows, cols, 0)
+    near = swapped(face0, "gy", lambda i: i ^ 1)
+    face1 = faces(field, rows, cols, 1)
     once0 = sweep_once(field, 0, half, rows, cols)
-    got_first, once0 = tied((got_first, once0))
-    second = second.at[2 * rows :].add(got_first[2 * rows :])
-    got_second = swapped(second, "gz", lambda i: i ^ 1)
-    once1 = sweep_once(field, half, half, rows, cols)
-    got_second, once1 = tied((got_second, once1))
-    counts = second[2 * rows :] + got_second[2 * rows :]
-    tiles, half0 = sweep_again_low(once0, rows, cols)
-    face1, tiles = tied((face1, tiles))
-    far = swapped(face1, "gy", lambda i: i ^ 1)
-    lowered, half1 = sweep_again_high(once1, tiles)
-
-    more = jnp.zeros_like(counts)
+
+    counts = first[2 * rows :]
     mask = columns // 2
     while mask > 1:
-        counts = counts + more
         more = swapped(counts, "gy", lambda i: i ^ mask)
         if mask == 4:
-            more, half0 = tied((more, half0))
+            more, face1 = tied((more, face1))
         if mask == 2:
-            more, half1 = tied((more, half1))
+            more, once0 = tied((more, once0))
+        counts = counts + more
         mask //= 2
+    face1, counts = tied((face1, counts))
+    far = swapped(face1, "gy", after_odd)
+
+    first = first.at[2 * rows :].set(counts)
+    got_first = swapped(first, "gz", after_odd)
+    once1 = sweep_once(field, half, half, rows, cols)
+    tiles, half0 = sweep_again_low(once0, rows, cols)
+    got_first, tiles = tied((got_first, tiles))
+    counts = counts + got_first[2 * rows :]
+    second = second.at[2 * rows :].set(counts)
+    got_second = swapped(second, "gz", lambda i: i ^ 1)
+    lowered, half1 = sweep_again_high(once1, tiles)
+    got_second, half1 = tied((got_second, half1))
+    more = got_second[2 * rows :]
     clow, chigh, counts = corners(got_first, got_second, counts, more)
     from_low = shifted(chigh, "gy", 1)
     from_high = shifted(clow, "gy", -1)

time: 41.8 us -> 47.1 us (1.13); the launches traced: 41.6 us -> 46.4 us
  waiting for transfers between devices: 7.51 us -> 11.3 us
  starting transfers between devices: 16 us -> 17 us
    ppermute x8, waiting for transfers between devices: 7.51 us -> 11.3 us  [swapped(): lax.ppermute(value, axis, [(i, partner(i) % count) for i in range(count)])]
    ppermute x8, starting transfers between devices: 16 us -> 17 us  [swapped(): lax.ppermute(value, axis, [(i, partner(i) % count) for i in range(count)])]
  transfers between devices with their start and end apart: 8 -> 8, of which waited for: 3 -> 3; matrix products, arithmetic and copies ran while one was open for 0% -> 0% of each run, Pallas kernels for 23% -> 21%
where the time goes in v3:
time: 47.1 us; the launch traced here: 46.4 us
  Pallas kernels  17.3 us (37%)
  starting transfers between devices  17 us (36%)
  waiting for transfers between devices  11.3 us (24%)
  between operations  0.8 us (2%)
    ppermute x8, starting transfers between devices, swapped(): lax.ppermute(value, axis, [(i, partner(i) % count) for i in range(count)])  17 us
    ppermute x8, waiting for transfers between devices, swapped(): lax.ppermute(value, axis, [(i, partner(i) % count) for i in range(count)])  11.3 us
    pallas_call x1, Pallas kernels, raise_all(): pl.pallas_call(raise_kernel, name='raise_all', out_shape=(jax.ShapeDtypeS...  6.25 us
    pallas_call x2, Pallas kernels, sweep_once(): pl.pallas_call(functools.partial(sweep_once_kernel, start, count, rows, c...  2.97 us
    pallas_call x1, Pallas kernels, sweep_again_high(): pl.pallas_call(sweep_again_high_kernel, name='sweep_again_high', out_shap...  2.05 us
    pallas_call x2, Pallas kernels, faces(): pl.pallas_call(functools.partial(faces_kernel, rows, cols, toward_odd), o...  1.64 us
    pallas_call x1, Pallas kernels, patch_far(): pl.pallas_call(functools.partial(patch_far_kernel, scale, lax.axis_size('...  1.41 us
    pallas_call x1, Pallas kernels, sweep_again_low(): pl.pallas_call(sweep_again_low_kernel, name='sweep_again_low', out_shape=...  1.39 us
  transfers between devices with their start and end apart: 8, of which 3 were waited for; matrix products, arithmetic and copies ran while one was open for 0% of the time, Pallas kernels for 21%

profile of v3, /device:TPU:0, one launch (start us, length us, event | category | flops | bytes accessed | tf_op | source)
XLA Modules:
  0.0 46.4 jit_solution(5407003824638561199)
XLA Ops:
  0.6 6.3 %raise_all.1 = (f32[66,200,128]{2,1,0:T(8,128)S(1)}, f32[40,1024]{1,0:T(8,128)S(1)}, f32[40,1024]{1,0:T(8,128)S(1)}) custom-call(f32[64,16,1024]{2,1,0:T(8,128)} %dist.1, s32[64,16,1024]{2,1,0:T(8,128)} %par.1, s32[32,128]{1,0:T(8,128)} %bitcast.2, s32[64,16,1024]{2,1,0:T(8,128)} %occ.1), custom_call_target="tpu_custom_call" | custom-call | bytes 12582912 | tf_op jit(solution)/shard_map/raise_all/pallas_call | solution.py:239
  6.9 4.1 %collective-permute-start = (f32[8,1024]{1,0:T(8,128)S(1)}, f32[8,1024]{1,0:T(8,128)S(1)}, u32[]{:S(2)}, u32[]{:S(2)}) collective-permute-start(f32[8,1024]{1,0:T(8,128)S(1)} %slice.43), channel_id=1, source_target_pairs={{0,4},{1,5},{2,6},{3,7},{4,0},{5,1},{6,2},{7,3},{8,12},{9,13},{10,... | collective-permute-start | bytes 98312 | tf_op jit(solution)/shard_map/ppermute | solution.py:569
  11.0 0.8 %shard_map.59 = f32[2,64,1024]{2,1,0:T(8,128)S(1)} custom-call(f32[66,200,128]{2,1,0:T(8,128)S(1)} %get-tuple-element.51.field), custom_call_target="tpu_custom_call" | custom-call | bytes 2097152 | tf_op jit(solution)/shard_map/pallas_call | solution.py:136
  11.9 1.4 %collective-permute-done = f32[8,1024]{1,0:T(8,128)S(1)} collective-permute-done((f32[8,1024]{1,0:T(8,128)S(1)}, f32[8,1024]{1,0:T(8,128)S(1)}, u32[]{:S(2)}, u32[]{:S(2)}) %collective-permute-start) | collective-permute-done | bytes 32800 | tf_op jit(solution)/shard_map/ppermute | solution.py:569
  13.3 1.6 %collective-permute-start.1 = (f32[8,1024]{1,0:T(8,128)S(1)}, f32[8,1024]{1,0:T(8,128)S(1)}, u32[]{:S(2)}, u32[]{:S(2)}) collective-permute-start(f32[8,1024]{1,0:T(8,128)S(1)} %slice_add_fusion.1), channel_id=1, source_target_pairs={{0,2},{1,3},{2,0},{3,1},{4,6},{5,7},{6,4},{7,5},{8,10},{9,11},{10,... | collective-permute-start | bytes 98312 | tf_op jit(solution)/shard_map/ppermute | solution.py:569
  14.8 1.5 %shard_map.60.once = f32[34,200,128]{2,1,0:T(8,128)S(1)} custom-call(f32[66,200,128]{2,1,0:T(8,128)S(1)} %get-tuple-element.51.field), custom_call_target="tpu_custom_call" | custom-call | bytes 8388608 | tf_op jit(solution)/shard_map/pallas_call | solution.py:281
  16.3 0.9 %collective-permute-done.1 = f32[8,1024]{1,0:T(8,128)S(1)} collective-permute-done((f32[8,1024]{1,0:T(8,128)S(1)}, f32[8,1024]{1,0:T(8,128)S(1)}, u32[]{:S(2)}, u32[]{:S(2)}) %collective-permute-start.1) | collective-permute-done | bytes 32800 | tf_op jit(solution)/shard_map/ppermute | solution.py:569
  17.2 0.1 collective-permute-start.2
  17.3 0.8 %shard_map.62 = f32[2,64,1024]{2,1,0:T(8,128)S(1)} custom-call(f32[66,200,128]{2,1,0:T(8,128)S(1)} %get-tuple-element.51.field), custom_call_target="tpu_custom_call" | custom-call | bytes 2097152 | tf_op jit(solution)/shard_map/pallas_call | solution.py:136
  18.1 1.8 %collective-permute-start.4 = (f32[2,64,1024]{2,1,0:T(8,128)S(1)}, f32[2,64,1024]{2,1,0:T(8,128)S(1)}, u32[]{:S(2)}, u32[]{:S(2)}) collective-permute-start(f32[2,64,1024]{2,1,0:T(8,128)S(1)} %shard_map.62), channel_id=1, source_target_pairs={{0,1},{1,0},{2,3},{3,2},{4,5},{5,4},{6,7},{7,6},{8,9},{9,8},{10,11... | collective-permute-start | bytes 1572872 | tf_op jit(solution)/shard_map/ppermute | solution.py:569
  19.9 3.6 %collective-permute-start.5 = (f32[2,64,1024]{2,1,0:T(8,128)S(1)}, f32[2,64,1024]{2,1,0:T(8,128)S(1)}, u32[]{:S(2)}, u32[]{:S(2)}) collective-permute-start(f32[2,64,1024]{2,1,0:T(8,128)S(1)} %shard_map.59), channel_id=1, source_target_pairs={{0,7},{1,2},{2,1},{3,4},{4,3},{5,6},{6,5},{7,0},{8,15},{9,10},{10,... | collective-permute-start | bytes 1572872 | tf_op jit(solution)/shard_map/ppermute | solution.py:569
  23.5 1.4 %sweep_again_low.1 = (f32[32,16,1024]{2,1,0:T(8,128)S(1)}, f32[4096,128]{1,0:T(8,128)S(1)}) custom-call(f32[34,200,128]{2,1,0:T(8,128)S(1)} %shard_map.60.once), custom_call_target="tpu_custom_call" | custom-call | bytes 8388608 | tf_op jit(solution)/shard_map/sweep_again_low/pallas_call | solution.py:333
  24.9 0.0 collective-permute-done.2.first
  24.9 1.1 %collective-permute-start.3 = (f32[40,1024]{1,0:T(8,128)S(1)}, f32[40,1024]{1,0:T(8,128)S(1)}, u32[]{:S(2)}, u32[]{:S(2)}) collective-permute-start(f32[40,1024]{1,0:T(8,128)S(1)} %get-tuple-element.74), channel_id=1, source_target_pairs={{0,8},{8,0},{16,24},{24,16},{1,9},{9,1},{17,25},{25,17},{2,10},{10... | collective-permute-start | bytes 491528 | tf_op jit(solution)/shard_map/ppermute | solution.py:569
  26.0 1.5 %shard_map.61.once = f32[34,200,128]{2,1,0:T(8,128)S(1)} custom-call(f32[66,200,128]{2,1,0:T(8,128)S(1)} %get-tuple-element.51.field), custom_call_target="tpu_custom_call" | custom-call | bytes 8388608 | tf_op jit(solution)/shard_map/pallas_call | solution.py:281
  27.5 2.0 %sweep_again_high.1 = (f32[64,16,1024]{2,1,0:T(8,128)}, f32[4096,128]{1,0:T(8,128)S(1)}) custom-call(f32[34,200,128]{2,1,0:T(8,128)S(1)} %shard_map.61.once, f32[32,16,1024]{2,1,0:T(8,128)S(1)} %get-tuple-element.60.low), custom_call_target="tpu_custom_call" | custom-call | bytes 8388608 | tf_op jit(solution)/shard_map/sweep_again_high/pallas_call | solution.py:350
  29.5 0.0 collective-permute-done.3.second
  29.6 0.1 collective-permute-start.6
  29.7 4.7 %collective-permute-start.7 = (f32[8,1024]{1,0:T(8,128)S(1)}, f32[8,1024]{1,0:T(8,128)S(1)}, u32[]{:S(2)}, u32[]{:S(2)}) collective-permute-start(f32[8,1024]{1,0:T(8,128)S(1)} %get-tuple-element.69), channel_id=1, source_target_pairs={{0,7},{1,0},{2,1},{3,2},{4,3},{5,4},{6,5},{7,6},{8,15},{9,8},{10,9... | collective-permute-start | bytes 98312 | tf_op jit(solution)/shard_map/ppermute | solution.py:569
  34.4 0.8 %patch_z.1 = (f32[64,16,1024]{2,1,0:T(8,128)}, f32[4,64,1024]{2,1,0:T(8,128)S(1)}) custom-call(f32[40,1024]{1,0:T(8,128)S(1)} %collective-permute-done.2.first, f32[40,1024]{1,0:T(8,128)S(1)} %collective-permute-done.3.second, f32[4096,128]{1,0:T(8,128)S(1)} %get-tuple-element.63.slab_low, ...), custom_call_target="tpu_custom_call", output_to_operand_aliasing={{0}: (4, {})} | custom-call | bytes 1048576 | tf_op jit(solution)/shard_map/patch_z/pallas_call | solution.py:438
  35.1 9.0 %collective-permute-done.4.near = f32[2,64,1024]{2,1,0:T(8,128)S(1)} collective-permute-done((f32[2,64,1024]{2,1,0:T(8,128)S(1)}, f32[2,64,1024]{2,1,0:T(8,128)S(1)}, u32[]{:S(2)}, u32[]{:S(2)}) %collective-permute-start.4) | collective-permute-done | bytes 524320 | tf_op jit(solution)/shard_map/ppermute | solution.py:569
  44.1 0.8 %patch_near.1._ = f32[64,16,1024]{2,1,0:T(8,128)} custom-call(f32[4,64,1024]{2,1,0:T(8,128)S(1)} %get-tuple-element.66.edges, f32[2,64,1024]{2,1,0:T(8,128)S(1)} %collective-permute-done.4.near, f32[64,16,1024]{2,1,0:T(8,128)} %get-tuple-element.71._), custom_call_target="tpu_custom_call", output_to_operand_aliasing={{}: (2, {})} | custom-call | bytes 1048576 | tf_op jit(solution)/shard_map/patch_near/pallas_call | solution.py:532
  45.0 0.0 collective-permute-done.6.clow
  45.0 0.0 collective-permute-done.7.chigh
  45.0 0.0 collective-permute-done.5.far
  45.0 1.4 %patch_far.1 = (f32[64,16,1024]{2,1,0:T(8,128)}, f32[1,1]{1,0:T(1,128)}) custom-call(f32[4,64,1024]{2,1,0:T(8,128)S(1)} %get-tuple-element.66.edges, f32[2,64,1024]{2,1,0:T(8,128)S(1)} %collective-permute-done.4.near, f32[2,64,1024]{2,1,0:T(8,128)S(1)} %collective-permute-done.5.far, ...), custom_call_target="tpu_custom_call", output_to_operand_aliasing={{0}: (6, {})} | custom-call | bytes 1048576 | tf_op jit(solution)/shard_map/patch_far/pallas_call | solution.py:547
  (7 shorter events, 0.1 us)
Async XLA Ops:
  6.9 6.4 %collective-permute-start = (f32[8,1024]{1,0:T(8,128)S(1)}, f32[8,1024]{1,0:T(8,128)S(1)}, u32[]{:S(2)}, u32[]{:S(2)}) collective-permute-start(f32[8,1024]{1,0:T(8,128)S(1)} %slice.43), channel_id=1, source_target_pairs={{0,4},{1,5},{2,6},{3,7},{4,0},{5,1},{6,2},{7,3},{8,12},{9,13},{10,... | collective-permute-start | bytes 98312 | tf_op jit(solution)/shard_map/ppermute | solution.py:569
  13.3 3.9 %collective-permute-start.1 = (f32[8,1024]{1,0:T(8,128)S(1)}, f32[8,1024]{1,0:T(8,128)S(1)}, u32[]{:S(2)}, u32[]{:S(2)}) collective-permute-start(f32[8,1024]{1,0:T(8,128)S(1)} %slice_add_fusion.1), channel_id=1, source_target_pairs={{0,2},{1,3},{2,0},{3,1},{4,6},{5,7},{6,4},{7,5},{8,10},{9,11},{10,... | collective-permute-start | bytes 98312 | tf_op jit(solution)/shard_map/ppermute | solution.py:569
  17.2 7.7 %collective-permute-start.2 = (f32[40,1024]{1,0:T(8,128)S(1)}, f32[40,1024]{1,0:T(8,128)S(1)}, u32[]{:S(2)}, u32[]{:S(2)}) collective-permute-start(f32[40,1024]{1,0:T(8,128)S(1)} %constant_dynamic-update-slice_fusion.1), channel_id=1, source_target_pairs={{0,24},{8,16},{16,8},{24,0},{1,25},{9,17},{17,9},{25,1},{2,26},{10... | collective-permute-start | bytes 491528 | tf_op jit(solution)/shard_map/ppermute | solution.py:569
  18.1 26.0 %collective-permute-start.4 = (f32[2,64,1024]{2,1,0:T(8,128)S(1)}, f32[2,64,1024]{2,1,0:T(8,128)S(1)}, u32[]{:S(2)}, u32[]{:S(2)}) collective-permute-start(f32[2,64,1024]{2,1,0:T(8,128)S(1)} %shard_map.62), channel_id=1, source_target_pairs={{0,1},{1,0},{2,3},{3,2},{4,5},{5,4},{6,7},{7,6},{8,9},{9,8},{10,11... | collective-permute-start | bytes 1572872 | tf_op jit(solution)/shard_map/ppermute | solution.py:569
  19.9 25.1 %collective-permute-start.5 = (f32[2,64,1024]{2,1,0:T(8,128)S(1)}, f32[2,64,1024]{2,1,0:T(8,128)S(1)}, u32[]{:S(2)}, u32[]{:S(2)}) collective-permute-start(f32[2,64,1024]{2,1,0:T(8,128)S(1)} %shard_map.59), channel_id=1, source_target_pairs={{0,7},{1,2},{2,1},{3,4},{4,3},{5,6},{6,5},{7,0},{8,15},{9,10},{10,... | collective-permute-start | bytes 1572872 | tf_op jit(solution)/shard_map/ppermute | solution.py:569
  24.9 4.6 %collective-permute-start.3 = (f32[40,1024]{1,0:T(8,128)S(1)}, f32[40,1024]{1,0:T(8,128)S(1)}, u32[]{:S(2)}, u32[]{:S(2)}) collective-permute-start(f32[40,1024]{1,0:T(8,128)S(1)} %get-tuple-element.74), channel_id=1, source_target_pairs={{0,8},{8,0},{16,24},{24,16},{1,9},{9,1},{17,25},{25,17},{2,10},{10... | collective-permute-start | bytes 491528 | tf_op jit(solution)/shard_map/ppermute | solution.py:569
  29.6 15.4 %collective-permute-start.6 = (f32[8,1024]{1,0:T(8,128)S(1)}, f32[8,1024]{1,0:T(8,128)S(1)}, u32[]{:S(2)}, u32[]{:S(2)}) collective-permute-start(f32[8,1024]{1,0:T(8,128)S(1)} %get-tuple-element.68), channel_id=1, source_target_pairs={{0,1},{1,2},{2,3},{3,4},{4,5},{5,6},{6,7},{7,0},{8,9},{9,10},{10,1... | collective-permute-start | bytes 98312 | tf_op jit(solution)/shard_map/ppermute | solution.py:569
  29.7 15.3 %collective-permute-start.7 = (f32[8,1024]{1,0:T(8,128)S(1)}, f32[8,1024]{1,0:T(8,128)S(1)}, u32[]{:S(2)}, u32[]{:S(2)}) collective-permute-start(f32[8,1024]{1,0:T(8,128)S(1)} %get-tuple-element.69), channel_id=1, source_target_pairs={{0,7},{1,0},{2,1},{3,2},{4,3},{5,4},{6,5},{7,6},{8,15},{9,8},{10,9... | collective-permute-start | bytes 98312 | tf_op jit(solution)/shard_map/ppermute | solution.py:569

commit v4 on v3

--- a/solution.py
+++ b/solution.py
@@ -207,7 +207,7 @@
             out[pl.ds(rows + y, SUBLANES), x] = swept[column]
 
 
-def raise_kernel(dist, par, flags_at, occ, field, first, second, flags, buf, ends, fsem, sem):
+def raise_kernel(dist, par, flags_at, occ, field, first, second, counts, flags, buf, ends, fsem, sem):
     depth, rows, cols = dist.shape
     total = raise_planes(0, depth, dist, par, flags_at, occ, field, flags, buf, fsem, sem)
     keep_end(field, 0, 1, rows, cols, ends.at[0])
@@ -216,11 +216,10 @@
     row = lax.broadcasted_iota(jnp.int32, (SUBLANES, cols), 0)
     small = (count & (2**COUNT_BITS - 1)).astype(jnp.float32)
     large = (count >> COUNT_BITS).astype(jnp.float32)
-    counts = jnp.where(row == 2, small, jnp.where(row == 3, large, 0.0))
+    counts[...] = jnp.where(row == 2, small, jnp.where(row == 3, large, 0.0))
     odd = lax.axis_index("gz") & 1
     for out, side in ((first, odd), (second, 1 - odd)):
-        out[pl.ds(0, 2 * rows), :] = ends[side]
-        out[pl.ds(2 * rows, SUBLANES), :] = counts
+        out[...] = ends[side]
 
 
 def raise_scratch(count, dist, par, flags, occ):
@@ -234,7 +233,7 @@
 
 def raise_all(dist, par, flags, occ):
     depth, rows, cols = dist.shape
-    message = jax.ShapeDtypeStruct((2 * rows + SUBLANES, cols), jnp.float32)
+    message = jax.ShapeDtypeStruct((2 * rows, cols), jnp.float32)
     scratch = raise_scratch(depth, dist, par, flags, occ)
     return pl.pallas_call(
         raise_kernel,
@@ -243,9 +242,10 @@
             jax.ShapeDtypeStruct((depth + 2, padded_rows(rows, cols), LANES), jnp.float32),
             message,
             message,
+            jax.ShapeDtypeStruct((SUBLANES, cols), jnp.float32),
         ),
         in_specs=[HBM] * 4,
-        out_specs=(VMEM,) * 3,
+        out_specs=(VMEM,) * 4,
         scratch_shapes=scratch[:2] + [pltpu.VMEM((2, 2 * rows, cols), jnp.float32)] + scratch[2:],
         compiler_params=params(20),
         cost_estimate=cost(12),
@@ -366,7 +366,7 @@
 
 
 def corners_kernel(first, second, counts, more, low, high, total):
-    rows = (first.shape[0] - SUBLANES) // 2
+    rows = first.shape[0] // 2
     odd = lax.axis_index("gz") & 1
     total[...] = counts[...] + more[...]
     low[...] = total[...]
@@ -586,13 +586,14 @@
         pltpu.with_memory_space_constraint(a, pltpu.HBM)
         for a in (distance, parent, removed.reshape(-1, LANES), occupied)
     )
-    field, first, second = raise_all(distance, parent, flags, occupied)
+    field, first, second, counts = raise_all(distance, parent, flags, occupied)
     face0 = faces(field, rows, cols, 0)
     near = swapped(face0, "gy", lambda i: i ^ 1)
+    got_first = swapped(first, "gz", after_odd)
+    got_second = swapped(second, "gz", lambda i: i ^ 1)
     face1 = faces(field, rows, cols, 1)
     once0 = sweep_once(field, 0, half, rows, cols)
 
-    counts = first[2 * rows :]
     mask = columns // 2
     while mask > 1:
         more = swapped(counts, "gy", lambda i: i ^ mask)
@@ -605,17 +606,14 @@
     face1, counts = tied((face1, counts))
     far = swapped(face1, "gy", after_odd)
 
-    first = first.at[2 * rows :].set(counts)
-    got_first = swapped(first, "gz", after_odd)
+    more = swapped(counts, "gz", after_odd)
     once1 = sweep_once(field, half, half, rows, cols)
     tiles, half0 = sweep_again_low(once0, rows, cols)
-    got_first, tiles = tied((got_first, tiles))
-    counts = counts + got_first[2 * rows :]
-    second = second.at[2 * rows :].set(counts)
-    got_second = swapped(second, "gz", lambda i: i ^ 1)
+    more, tiles = tied((more, tiles))
+    counts = counts + more
+    more = swapped(counts, "gz", lambda i: i ^ 1)
     lowered, half1 = sweep_again_high(once1, tiles)
-    got_second, half1 = tied((got_second, half1))
-    more = got_second[2 * rows :]
+    more, half1 = tied((more, half1))
     clow, chigh, counts = corners(got_first, got_second, counts, more)
     from_low = shifted(chigh, "gy", 1)
     from_high = shifted(clow, "gy", -1)

time: 47.1 us -> 42.8 us (0.909); the launches traced: 46.4 us -> 42.6 us
  waiting for transfers between devices: 11.3 us -> 7.36 us
    ppermute x8 -> x10, waiting for transfers between devices: 11.3 us -> 7.36 us  [swapped(): lax.ppermute(value, axis, [(i, partner(i) % count) for i in range(count)])]
    ppermute x8 -> x10, starting transfers between devices: 17 us -> 17.2 us  [swapped(): lax.ppermute(value, axis, [(i, partner(i) % count) for i in range(count)])]
  transfers between devices with their start and end apart: 8 -> 10, of which waited for: 3 -> 3; matrix products, arithmetic and copies ran while one was open for 0% -> 0% of each run, Pallas kernels for 21% -> 23%
where the time goes in v4:
time: 42.8 us; the launch traced here: 42.6 us
  Pallas kernels  17.3 us (40%)
  starting transfers between devices  17.2 us (40%)
  waiting for transfers between devices  7.36 us (17%)
  between operations  0.79 us (2%)
    ppermute x10, starting transfers between devices, swapped(): lax.ppermute(value, axis, [(i, partner(i) % count) for i in range(count)])  17.2 us
    ppermute x10, waiting for transfers between devices, swapped(): lax.ppermute(value, axis, [(i, partner(i) % count) for i in range(count)])  7.36 us
    pallas_call x1, Pallas kernels, raise_all(): pl.pallas_call(raise_kernel, name='raise_all', out_shape=(jax.ShapeDtypeS...  6.25 us
    pallas_call x2, Pallas kernels, sweep_once(): pl.pallas_call(functools.partial(sweep_once_kernel, start, count, rows, c...  2.97 us
    pallas_call x1, Pallas kernels, sweep_again_high(): pl.pallas_call(sweep_again_high_kernel, name='sweep_again_high', out_shap...  2.05 us
    pallas_call x2, Pallas kernels, faces(): pl.pallas_call(functools.partial(faces_kernel, rows, cols, toward_odd), o...  1.63 us
    pallas_call x1, Pallas kernels, patch_far(): pl.pallas_call(functools.partial(patch_far_kernel, scale, lax.axis_size('...  1.41 us
    pallas_call x1, Pallas kernels, sweep_again_low(): pl.pallas_call(sweep_again_low_kernel, name='sweep_again_low', out_shape=...  1.39 us
  transfers between devices with their start and end apart: 10, of which 3 were waited for; matrix products, arithmetic and copies ran while one was open for 0% of the time, Pallas kernels for 23%

profile of v4, /device:TPU:0, one launch (start us, length us, event | category | flops | bytes accessed | tf_op | source)
XLA Modules:
  0.0 42.6 jit_solution(615496488474007387)
XLA Ops:
  0.6 6.3 %raise_all.1 = (f32[66,200,128]{2,1,0:T(8,128)S(1)}, f32[32,1024]{1,0:T(8,128)S(1)}, f32[32,1024]{1,0:T(8,128)S(1)}, f32[8,1024]{1,0:T(8,128)S(1)}) custom-call(f32[64,16,1024]{2,1,0:T(8,128)} %dist.1, s32[64,16,1024]{2,1,0:T(8,128)} %par.1, s32[32,128]{1,0:T(8,128)} %bitcast.2, s32[64,16,1024]{2,1,0:T(8,128)} %occ.1), custom_call_target="tpu_custom_call" | custom-call | bytes 12582912 | tf_op jit(solution)/shard_map/raise_all/pallas_call | solution.py:238
  6.9 4.1 %collective-permute-start.2 = (f32[8,1024]{1,0:T(8,128)S(1)}, f32[8,1024]{1,0:T(8,128)S(1)}, u32[]{:S(2)}, u32[]{:S(2)}) collective-permute-start(f32[8,1024]{1,0:T(8,128)S(1)} %get-tuple-element.29), channel_id=1, source_target_pairs={{0,4},{1,5},{2,6},{3,7},{4,0},{5,1},{6,2},{7,3},{8,12},{9,13},{10,... | collective-permute-start | bytes 98312 | tf_op jit(solution)/shard_map/ppermute | solution.py:569
  11.0 0.8 %shard_map.59 = f32[2,64,1024]{2,1,0:T(8,128)S(1)} custom-call(f32[66,200,128]{2,1,0:T(8,128)S(1)} %get-tuple-element.30.field), custom_call_target="tpu_custom_call" | custom-call | bytes 2097152 | tf_op jit(solution)/shard_map/pallas_call | solution.py:136
  11.8 1.4 %collective-permute-done.2 = f32[8,1024]{1,0:T(8,128)S(1)} collective-permute-done((f32[8,1024]{1,0:T(8,128)S(1)}, f32[8,1024]{1,0:T(8,128)S(1)}, u32[]{:S(2)}, u32[]{:S(2)}) %collective-permute-start.2) | collective-permute-done | bytes 32800 | tf_op jit(solution)/shard_map/ppermute | solution.py:569
  13.3 1.6 %collective-permute-start.3 = (f32[8,1024]{1,0:T(8,128)S(1)}, f32[8,1024]{1,0:T(8,128)S(1)}, u32[]{:S(2)}, u32[]{:S(2)}) collective-permute-start(f32[8,1024]{1,0:T(8,128)S(1)} %add.9), channel_id=1, source_target_pairs={{0,2},{1,3},{2,0},{3,1},{4,6},{5,7},{6,4},{7,5},{8,10},{9,11},{10,... | collective-permute-start | bytes 98312 | tf_op jit(solution)/shard_map/ppermute | solution.py:569
  14.8 0.8 %shard_map.62 = f32[2,64,1024]{2,1,0:T(8,128)S(1)} custom-call(f32[66,200,128]{2,1,0:T(8,128)S(1)} %get-tuple-element.30.field), custom_call_target="tpu_custom_call" | custom-call | bytes 2097152 | tf_op jit(solution)/shard_map/pallas_call | solution.py:136
  15.7 1.6 %collective-permute-start.6 = (f32[2,64,1024]{2,1,0:T(8,128)S(1)}, f32[2,64,1024]{2,1,0:T(8,128)S(1)}, u32[]{:S(2)}, u32[]{:S(2)}) collective-permute-start(f32[2,64,1024]{2,1,0:T(8,128)S(1)} %shard_map.62), channel_id=1, source_target_pairs={{0,1},{1,0},{2,3},{3,2},{4,5},{5,4},{6,7},{7,6},{8,9},{9,8},{10,11... | collective-permute-start | bytes 1572872 | tf_op jit(solution)/shard_map/ppermute | solution.py:569
  17.2 1.5 %shard_map.60.once = f32[34,200,128]{2,1,0:T(8,128)S(1)} custom-call(f32[66,200,128]{2,1,0:T(8,128)S(1)} %get-tuple-element.30.field), custom_call_target="tpu_custom_call" | custom-call | bytes 8388608 | tf_op jit(solution)/shard_map/pallas_call | solution.py:281
  18.7 0.0 collective-permute-done.3
  18.8 3.2 %collective-permute-start.7 = (f32[2,64,1024]{2,1,0:T(8,128)S(1)}, f32[2,64,1024]{2,1,0:T(8,128)S(1)}, u32[]{:S(2)}, u32[]{:S(2)}) collective-permute-start(f32[2,64,1024]{2,1,0:T(8,128)S(1)} %shard_map.59), channel_id=1, source_target_pairs={{0,7},{1,2},{2,1},{3,4},{4,3},{5,6},{6,5},{7,0},{8,15},{9,10},{10,... | collective-permute-start | bytes 1572872 | tf_op jit(solution)/shard_map/ppermute | solution.py:569
  22.0 0.0 collective-permute-start
  22.0 1.6 %collective-permute-start.1 = (f32[32,1024]{1,0:T(8,128)S(1)}, f32[32,1024]{1,0:T(8,128)S(1)}, u32[]{:S(2)}, u32[]{:S(2)}) collective-permute-start(f32[32,1024]{1,0:T(8,128)S(1)} %get-tuple-element.28), channel_id=1, source_target_pairs={{0,8},{8,0},{16,24},{24,16},{1,9},{9,1},{17,25},{25,17},{2,10},{10... | collective-permute-start | bytes 393224 | tf_op jit(solution)/shard_map/ppermute | solution.py:569
  23.6 0.1 collective-permute-start.4
  23.7 1.4 %sweep_again_low.1 = (f32[32,16,1024]{2,1,0:T(8,128)S(1)}, f32[4096,128]{1,0:T(8,128)S(1)}) custom-call(f32[34,200,128]{2,1,0:T(8,128)S(1)} %shard_map.60.once), custom_call_target="tpu_custom_call" | custom-call | bytes 8388608 | tf_op jit(solution)/shard_map/sweep_again_low/pallas_call | solution.py:333
  25.1 3.3 %collective-permute-done.4 = f32[8,1024]{1,0:T(8,128)S(1)} collective-permute-done((f32[8,1024]{1,0:T(8,128)S(1)}, f32[8,1024]{1,0:T(8,128)S(1)}, u32[]{:S(2)}, u32[]{:S(2)}) %collective-permute-start.4) | collective-permute-done | bytes 32800 | tf_op jit(solution)/shard_map/ppermute | solution.py:569
  28.4 0.2 collective-permute-start.5
  28.6 1.5 %shard_map.61.once = f32[34,200,128]{2,1,0:T(8,128)S(1)} custom-call(f32[66,200,128]{2,1,0:T(8,128)S(1)} %get-tuple-element.30.field), custom_call_target="tpu_custom_call" | custom-call | bytes 8388608 | tf_op jit(solution)/shard_map/pallas_call | solution.py:281
  30.1 2.0 %sweep_again_high.1 = (f32[64,16,1024]{2,1,0:T(8,128)}, f32[4096,128]{1,0:T(8,128)S(1)}) custom-call(f32[34,200,128]{2,1,0:T(8,128)S(1)} %shard_map.61.once, f32[32,16,1024]{2,1,0:T(8,128)S(1)} %get-tuple-element.39.low), custom_call_target="tpu_custom_call" | custom-call | bytes 8388608 | tf_op jit(solution)/shard_map/sweep_again_high/pallas_call | solution.py:350
  32.1 0.0 collective-permute-done.5.more
  32.1 0.0 collective-permute-done.first
  32.2 0.0 collective-permute-done.1.second
  32.2 0.1 collective-permute-start.8
  32.3 4.7 %collective-permute-start.9 = (f32[8,1024]{1,0:T(8,128)S(1)}, f32[8,1024]{1,0:T(8,128)S(1)}, u32[]{:S(2)}, u32[]{:S(2)}) collective-permute-start(f32[8,1024]{1,0:T(8,128)S(1)} %get-tuple-element.47), channel_id=1, source_target_pairs={{0,7},{1,0},{2,1},{3,2},{4,3},{5,4},{6,5},{7,6},{8,15},{9,8},{10,9... | collective-permute-start | bytes 98312 | tf_op jit(solution)/shard_map/ppermute | solution.py:569
  37.0 0.8 %patch_z.1 = (f32[64,16,1024]{2,1,0:T(8,128)}, f32[4,64,1024]{2,1,0:T(8,128)S(1)}) custom-call(f32[32,1024]{1,0:T(8,128)S(1)} %collective-permute-done.first, f32[32,1024]{1,0:T(8,128)S(1)} %collective-permute-done.1.second, f32[4096,128]{1,0:T(8,128)S(1)} %get-tuple-element.33.slab_low, ...), custom_call_target="tpu_custom_call", output_to_operand_aliasing={{0}: (4, {})} | custom-call | bytes 1048576 | tf_op jit(solution)/shard_map/patch_z/pallas_call | solution.py:438
  37.7 2.6 %collective-permute-done.6.near = f32[2,64,1024]{2,1,0:T(8,128)S(1)} collective-permute-done((f32[2,64,1024]{2,1,0:T(8,128)S(1)}, f32[2,64,1024]{2,1,0:T(8,128)S(1)}, u32[]{:S(2)}, u32[]{:S(2)}) %collective-permute-start.6) | collective-permute-done | bytes 524320 | tf_op jit(solution)/shard_map/ppermute | solution.py:569
  40.3 0.8 %patch_near.1._ = f32[64,16,1024]{2,1,0:T(8,128)} custom-call(f32[4,64,1024]{2,1,0:T(8,128)S(1)} %get-tuple-element.43.edges, f32[2,64,1024]{2,1,0:T(8,128)S(1)} %collective-permute-done.6.near, f32[64,16,1024]{2,1,0:T(8,128)} %get-tuple-element.49._), custom_call_target="tpu_custom_call", output_to_operand_aliasing={{}: (2, {})} | custom-call | bytes 1048576 | tf_op jit(solution)/shard_map/patch_near/pallas_call | solution.py:532
  41.2 0.0 collective-permute-done.8.clow
  41.2 0.0 collective-permute-done.9.chigh
  41.2 0.0 collective-permute-done.7.far
  41.2 1.4 %patch_far.1 = (f32[64,16,1024]{2,1,0:T(8,128)}, f32[1,1]{1,0:T(1,128)}) custom-call(f32[4,64,1024]{2,1,0:T(8,128)S(1)} %get-tuple-element.43.edges, f32[2,64,1024]{2,1,0:T(8,128)S(1)} %collective-permute-done.6.near, f32[2,64,1024]{2,1,0:T(8,128)S(1)} %collective-permute-done.7.far, ...), custom_call_target="tpu_custom_call", output_to_operand_aliasing={{0}: (6, {})} | custom-call | bytes 1048576 | tf_op jit(solution)/shard_map/patch_far/pallas_call | solution.py:547
  (4 shorter events, 0.0 us)
Async XLA Ops:
  6.9 6.4 %collective-permute-start.2 = (f32[8,1024]{1,0:T(8,128)S(1)}, f32[8,1024]{1,0:T(8,128)S(1)}, u32[]{:S(2)}, u32[]{:S(2)}) collective-permute-start(f32[8,1024]{1,0:T(8,128)S(1)} %get-tuple-element.29), channel_id=1, source_target_pairs={{0,4},{1,5},{2,6},{3,7},{4,0},{5,1},{6,2},{7,3},{8,12},{9,13},{10,... | collective-permute-start | bytes 98312 | tf_op jit(solution)/shard_map/ppermute | solution.py:569
  13.3 5.5 %collective-permute-start.3 = (f32[8,1024]{1,0:T(8,128)S(1)}, f32[8,1024]{1,0:T(8,128)S(1)}, u32[]{:S(2)}, u32[]{:S(2)}) collective-permute-start(f32[8,1024]{1,0:T(8,128)S(1)} %add.9), channel_id=1, source_target_pairs={{0,2},{1,3},{2,0},{3,1},{4,6},{5,7},{6,4},{7,5},{8,10},{9,11},{10,... | collective-permute-start | bytes 98312 | tf_op jit(solution)/shard_map/ppermute | solution.py:569
  15.7 24.7 %collective-permute-start.6 = (f32[2,64,1024]{2,1,0:T(8,128)S(1)}, f32[2,64,1024]{2,1,0:T(8,128)S(1)}, u32[]{:S(2)}, u32[]{:S(2)}) collective-permute-start(f32[2,64,1024]{2,1,0:T(8,128)S(1)} %shard_map.62), channel_id=1, source_target_pairs={{0,1},{1,0},{2,3},{3,2},{4,5},{5,4},{6,7},{7,6},{8,9},{9,8},{10,11... | collective-permute-start | bytes 1572872 | tf_op jit(solution)/shard_map/ppermute | solution.py:569
  18.8 22.5 %collective-permute-start.7 = (f32[2,64,1024]{2,1,0:T(8,128)S(1)}, f32[2,64,1024]{2,1,0:T(8,128)S(1)}, u32[]{:S(2)}, u32[]{:S(2)}) collective-permute-start(f32[2,64,1024]{2,1,0:T(8,128)S(1)} %shard_map.59), channel_id=1, source_target_pairs={{0,7},{1,2},{2,1},{3,4},{4,3},{5,6},{6,5},{7,0},{8,15},{9,10},{10,... | collective-permute-start | bytes 1572872 | tf_op jit(solution)/shard_map/ppermute | solution.py:569
  22.0 10.2 %collective-permute-start = (f32[32,1024]{1,0:T(8,128)S(1)}, f32[32,1024]{1,0:T(8,128)S(1)}, u32[]{:S(2)}, u32[]{:S(2)}) collective-permute-start(f32[32,1024]{1,0:T(8,128)S(1)} %get-tuple-element.27), channel_id=1, source_target_pairs={{0,24},{8,16},{16,8},{24,0},{1,25},{9,17},{17,9},{25,1},{2,26},{10... | collective-permute-start | bytes 393224 | tf_op jit(solution)/shard_map/ppermute | solution.py:569
  22.0 10.2 %collective-permute-start.1 = (f32[32,1024]{1,0:T(8,128)S(1)}, f32[32,1024]{1,0:T(8,128)S(1)}, u32[]{:S(2)}, u32[]{:S(2)}) collective-permute-start(f32[32,1024]{1,0:T(8,128)S(1)} %get-tuple-element.28), channel_id=1, source_target_pairs={{0,8},{8,0},{16,24},{24,16},{1,9},{9,1},{17,25},{25,17},{2,10},{10... | collective-permute-start | bytes 393224 | tf_op jit(solution)/shard_map/ppermute | solution.py:569
  23.6 4.8 %collective-permute-start.4 = (f32[8,1024]{1,0:T(8,128)S(1)}, f32[8,1024]{1,0:T(8,128)S(1)}, u32[]{:S(2)}, u32[]{:S(2)}) collective-permute-start(f32[8,1024]{1,0:T(8,128)S(1)} %add.10), channel_id=1, source_target_pairs={{0,24},{8,16},{16,8},{24,0},{1,25},{9,17},{17,9},{25,1},{2,26},{10... | collective-permute-start | bytes 98312 | tf_op jit(solution)/shard_map/ppermute | solution.py:569
  28.4 3.7 %collective-permute-start.5 = (f32[8,1024]{1,0:T(8,128)S(1)}, f32[8,1024]{1,0:T(8,128)S(1)}, u32[]{:S(2)}, u32[]{:S(2)}) collective-permute-start(f32[8,1024]{1,0:T(8,128)S(1)} %add.11.counts), channel_id=1, source_target_pairs={{0,8},{8,0},{16,24},{24,16},{1,9},{9,1},{17,25},{25,17},{2,10},{10... | collective-permute-start | bytes 98312 | tf_op jit(solution)/shard_map/ppermute | solution.py:569
  32.2 9.0 %collective-permute-start.8 = (f32[8,1024]{1,0:T(8,128)S(1)}, f32[8,1024]{1,0:T(8,128)S(1)}, u32[]{:S(2)}, u32[]{:S(2)}) collective-permute-start(f32[8,1024]{1,0:T(8,128)S(1)} %get-tuple-element.46), channel_id=1, source_target_pairs={{0,1},{1,2},{2,3},{3,4},{4,5},{5,6},{6,7},{7,0},{8,9},{9,10},{10,1... | collective-permute-start | bytes 98312 | tf_op jit(solution)/shard_map/ppermute | solution.py:569
  32.3 9.0 %collective-permute-start.9 = (f32[8,1024]{1,0:T(8,128)S(1)}, f32[8,1024]{1,0:T(8,128)S(1)}, u32[]{:S(2)}, u32[]{:S(2)}) collective-permute-start(f32[8,1024]{1,0:T(8,128)S(1)} %get-tuple-element.47), channel_id=1, source_target_pairs={{0,7},{1,0},{2,1},{3,2},{4,3},{5,4},{6,5},{7,6},{8,15},{9,8},{10,9... | collective-permute-start | bytes 98312 | tf_op jit(solution)/shard_map/ppermute | solution.py:569

commit v5 on v4

--- a/solution.py
+++ b/solution.py
@@ -470,52 +470,27 @@
     return (((0, 0), (1, 1)), ((rows - 1, 3), (rows - 2, 2)))
 
 
-def patch_near_kernel(edges, near, _, out, buf, sem):
-    odd = lax.axis_index("gy") & 1
-    for side, places in enumerate(sides(out.shape[1])):
-
-        @pl.when(odd == 1 - side)
-        def _():
-            copies = []
-            for away, (row, edge) in enumerate(places):
-                merge_rows(away, edges.at[edge], near, None, None, buf.at[away])
-                cp = pltpu.make_async_copy(buf.at[away], out.at[:, row, :], sem.at[away])
-                cp.start()
-                copies.append(cp)
-            for cp in copies:
-                cp.wait()
-
-
 def patch_far_kernel(
-    scale, slabs, edges, near, far, clow, chigh, counts, _, out, share, buf, lines, sem
+    scale, slabs, edges, near, far, clow, chigh, counts, _, out, share, buf, sem
 ):
-    depth, rows, _ = out.shape
+    _, rows, _ = out.shape
     odd = lax.axis_index("gy") & 1
     slab = lax.axis_index("gz")
     missing = (slab == 0, slab == slabs - 1)
     corners = (clow, chigh)
-    for side, places in enumerate(sides(rows)):
+    for side in range(2):
 
         @pl.when(odd == side)
         def _():
             copies = []
-            for away, (row, edge) in enumerate(places):
-                corner = None if away else corners[side]
-                merge_rows(away, edges.at[edge], far, corner, missing, buf.at[away])
-                cp = pltpu.make_async_copy(buf.at[away], out.at[:, row, :], sem.at[away])
-                cp.start()
-                copies.append(cp)
-            row, edge = sides(rows)[1 - side][0]
-            for end, z in enumerate((0, depth - 1)):
-                line = pl.ds(z, 1)
-                reach = jnp.minimum(edges[edge, line, :], near[1, line, :] + VOXEL)
-                offer = jnp.where(missing[end], FAR, corners[1 - side][pl.ds(end, 1), :])
-                lines[end] = jnp.minimum(reach, offer + VOXEL + VOXEL)
-                cp = pltpu.make_async_copy(
-                    lines.at[end], out.at[line, row, :], sem.at[2 + end]
-                )
-                cp.start()
-                copies.append(cp)
+            for face, end in ((near, 1 - side), (far, side)):
+                for away, (row, edge) in enumerate(sides(rows)[end]):
+                    corner = None if away else corners[end]
+                    at = len(copies)
+                    merge_rows(away, edges.at[edge], face, corner, missing, buf.at[at])
+                    cp = pltpu.make_async_copy(buf.at[at], out.at[:, row, :], sem.at[at])
+                    cp.start()
+                    copies.append(cp)
             for cp in copies:
                 cp.wait()
 
@@ -525,21 +500,6 @@
     both = jnp.where(row == 2, both, jnp.where(row == 3, both << COUNT_BITS, 0))
     count = jnp.sum(both, axis=0, keepdims=True)
     share[...] = count[:, :1].astype(jnp.float32) * jnp.float32(scale)
-
-
-def patch_near(edges, near, out):
-    depth, _, cols = out.shape
-    return pl.pallas_call(
-        patch_near_kernel,
-        name="patch_near",
-        out_shape=jax.ShapeDtypeStruct(out.shape, out.dtype),
-        in_specs=[VMEM] * 2 + [HBM],
-        out_specs=HBM,
-        input_output_aliases={2: 0},
-        scratch_shapes=[pltpu.VMEM((2, depth, cols), jnp.float32), pltpu.SemaphoreType.DMA((2,))],
-        compiler_params=params(4),
-        cost_estimate=cost(1),
-    )(edges, near, out)
 
 
 def patch_far(scale, edges, near, far, clow, chigh, counts, out):
@@ -555,8 +515,7 @@
         out_specs=(HBM, VMEM),
         input_output_aliases={6: 0},
         scratch_shapes=[
-            pltpu.VMEM((2, depth, cols), jnp.float32),
-            pltpu.VMEM((2, 1, cols), jnp.float32),
+            pltpu.VMEM((4, depth, cols), jnp.float32),
             pltpu.SemaphoreType.DMA((4,)),
         ],
         compiler_params=params(4),
@@ -619,7 +578,6 @@
     from_high = shifted(clow, "gy", -1)
     lowered, edges = patch_z(got_first, got_second, half0, half1, lowered)
     total = distance.size * slabs * columns
-    lowered = patch_near(edges, near, lowered)
     lowered, share = patch_far(
         100.0 / total, edges, near, far, from_low, from_high, counts, lowered
     )

time: 42.8 us -> 42.4 us (level)
  Pallas kernels: 17.3 us -> 16.6 us
    pallas_call x1 -> x0, Pallas kernels: 0.85 us -> none  [patch_near(): pl.pallas_call(patch_near_kernel, name='patch_near', out_shape=jax.ShapeD...]
  transfers between devices with their start and end apart: 10 -> 10, of which waited for: 3 -> 4; matrix products, arithmetic and copies ran while one was open for 0% -> 0% of each run, Pallas kernels for 23% -> 21%
where the time goes in v5:
time: 42.4 us; the launch traced here: 42.3 us
  starting transfers between devices  17.2 us (41%)
  Pallas kernels  16.6 us (39%)
  waiting for transfers between devices  7.71 us (18%)
  between operations  0.76 us (2%)
    ppermute x10, starting transfers between devices, swapped(): lax.ppermute(value, axis, [(i, partner(i) % count) for i in range(count)])  17.2 us
    ppermute x10, waiting for transfers between devices, swapped(): lax.ppermute(value, axis, [(i, partner(i) % count) for i in range(count)])  7.71 us
    pallas_call x1, Pallas kernels, raise_all(): pl.pallas_call(raise_kernel, name='raise_all', out_shape=(jax.ShapeDtypeS...  6.25 us
    pallas_call x2, Pallas kernels, sweep_once(): pl.pallas_call(functools.partial(sweep_once_kernel, start, count, rows, c...  2.97 us
    pallas_call x1, Pallas kernels, sweep_again_high(): pl.pallas_call(sweep_again_high_kernel, name='sweep_again_high', out_shap...  2.05 us
    pallas_call x2, Pallas kernels, faces(): pl.pallas_call(functools.partial(faces_kernel, rows, cols, toward_odd), o...  1.63 us
    pallas_call x1, Pallas kernels, patch_far(): pl.pallas_call(functools.partial(patch_far_kernel, scale, lax.axis_size('...  1.57 us
    pallas_call x1, Pallas kernels, sweep_again_low(): pl.pallas_call(sweep_again_low_kernel, name='sweep_again_low', out_shape=...  1.39 us
  transfers between devices with their start and end apart: 10, of which 4 were waited for; matrix products, arithmetic and copies ran while one was open for 0% of the time, Pallas kernels for 21%

profile of v5, /device:TPU:0, one launch (start us, length us, event | category | flops | bytes accessed | tf_op | source)
XLA Modules:
  0.0 42.3 jit_solution(15923116848262104443)
XLA Ops:
  0.6 6.3 %raise_all.1 = (f32[66,200,128]{2,1,0:T(8,128)S(1)}, f32[32,1024]{1,0:T(8,128)S(1)}, f32[32,1024]{1,0:T(8,128)S(1)}, f32[8,1024]{1,0:T(8,128)S(1)}) custom-call(f32[64,16,1024]{2,1,0:T(8,128)} %dist.1, s32[64,16,1024]{2,1,0:T(8,128)} %par.1, s32[32,128]{1,0:T(8,128)} %bitcast.2, s32[64,16,1024]{2,1,0:T(8,128)} %occ.1), custom_call_target="tpu_custom_call" | custom-call | bytes 12582912 | tf_op jit(solution)/shard_map/raise_all/pallas_call | solution.py:238
  6.9 4.1 %collective-permute-start.2 = (f32[8,1024]{1,0:T(8,128)S(1)}, f32[8,1024]{1,0:T(8,128)S(1)}, u32[]{:S(2)}, u32[]{:S(2)}) collective-permute-start(f32[8,1024]{1,0:T(8,128)S(1)} %get-tuple-element.29), channel_id=1, source_target_pairs={{0,4},{1,5},{2,6},{3,7},{4,0},{5,1},{6,2},{7,3},{8,12},{9,13},{10,... | collective-permute-start | bytes 98312 | tf_op jit(solution)/shard_map/ppermute | solution.py:528
  11.0 0.8 %shard_map.59 = f32[2,64,1024]{2,1,0:T(8,128)S(1)} custom-call(f32[66,200,128]{2,1,0:T(8,128)S(1)} %get-tuple-element.30.field), custom_call_target="tpu_custom_call" | custom-call | bytes 2097152 | tf_op jit(solution)/shard_map/pallas_call | solution.py:136
  11.8 1.4 %collective-permute-done.2 = f32[8,1024]{1,0:T(8,128)S(1)} collective-permute-done((f32[8,1024]{1,0:T(8,128)S(1)}, f32[8,1024]{1,0:T(8,128)S(1)}, u32[]{:S(2)}, u32[]{:S(2)}) %collective-permute-start.2) | collective-permute-done | bytes 32800 | tf_op jit(solution)/shard_map/ppermute | solution.py:528
  13.3 1.6 %collective-permute-start.3 = (f32[8,1024]{1,0:T(8,128)S(1)}, f32[8,1024]{1,0:T(8,128)S(1)}, u32[]{:S(2)}, u32[]{:S(2)}) collective-permute-start(f32[8,1024]{1,0:T(8,128)S(1)} %add.9), channel_id=1, source_target_pairs={{0,2},{1,3},{2,0},{3,1},{4,6},{5,7},{6,4},{7,5},{8,10},{9,11},{10,... | collective-permute-start | bytes 98312 | tf_op jit(solution)/shard_map/ppermute | solution.py:528
  14.8 0.8 %shard_map.62 = f32[2,64,1024]{2,1,0:T(8,128)S(1)} custom-call(f32[66,200,128]{2,1,0:T(8,128)S(1)} %get-tuple-element.30.field), custom_call_target="tpu_custom_call" | custom-call | bytes 2097152 | tf_op jit(solution)/shard_map/pallas_call | solution.py:136
  15.7 1.6 %collective-permute-start.6 = (f32[2,64,1024]{2,1,0:T(8,128)S(1)}, f32[2,64,1024]{2,1,0:T(8,128)S(1)}, u32[]{:S(2)}, u32[]{:S(2)}) collective-permute-start(f32[2,64,1024]{2,1,0:T(8,128)S(1)} %shard_map.62), channel_id=1, source_target_pairs={{0,1},{1,0},{2,3},{3,2},{4,5},{5,4},{6,7},{7,6},{8,9},{9,8},{10,11... | collective-permute-start | bytes 1572872 | tf_op jit(solution)/shard_map/ppermute | solution.py:528
  17.2 1.5 %shard_map.60.once = f32[34,200,128]{2,1,0:T(8,128)S(1)} custom-call(f32[66,200,128]{2,1,0:T(8,128)S(1)} %get-tuple-element.30.field), custom_call_target="tpu_custom_call" | custom-call | bytes 8388608 | tf_op jit(solution)/shard_map/pallas_call | solution.py:281
  18.7 0.0 collective-permute-done.3
  18.8 3.2 %collective-permute-start.7 = (f32[2,64,1024]{2,1,0:T(8,128)S(1)}, f32[2,64,1024]{2,1,0:T(8,128)S(1)}, u32[]{:S(2)}, u32[]{:S(2)}) collective-permute-start(f32[2,64,1024]{2,1,0:T(8,128)S(1)} %shard_map.59), channel_id=1, source_target_pairs={{0,7},{1,2},{2,1},{3,4},{4,3},{5,6},{6,5},{7,0},{8,15},{9,10},{10,... | collective-permute-start | bytes 1572872 | tf_op jit(solution)/shard_map/ppermute | solution.py:528
  22.0 0.0 collective-permute-start
  22.0 1.6 %collective-permute-start.1 = (f32[32,1024]{1,0:T(8,128)S(1)}, f32[32,1024]{1,0:T(8,128)S(1)}, u32[]{:S(2)}, u32[]{:S(2)}) collective-permute-start(f32[32,1024]{1,0:T(8,128)S(1)} %get-tuple-element.28), channel_id=1, source_target_pairs={{0,8},{8,0},{16,24},{24,16},{1,9},{9,1},{17,25},{25,17},{2,10},{10... | collective-permute-start | bytes 393224 | tf_op jit(solution)/shard_map/ppermute | solution.py:528
  23.6 0.1 collective-permute-start.4
  23.7 1.4 %sweep_again_low.1 = (f32[32,16,1024]{2,1,0:T(8,128)S(1)}, f32[4096,128]{1,0:T(8,128)S(1)}) custom-call(f32[34,200,128]{2,1,0:T(8,128)S(1)} %shard_map.60.once), custom_call_target="tpu_custom_call" | custom-call | bytes 8388608 | tf_op jit(solution)/shard_map/sweep_again_low/pallas_call | solution.py:333
  25.1 3.3 %collective-permute-done.4 = f32[8,1024]{1,0:T(8,128)S(1)} collective-permute-done((f32[8,1024]{1,0:T(8,128)S(1)}, f32[8,1024]{1,0:T(8,128)S(1)}, u32[]{:S(2)}, u32[]{:S(2)}) %collective-permute-start.4) | collective-permute-done | bytes 32800 | tf_op jit(solution)/shard_map/ppermute | solution.py:528
  28.4 0.2 collective-permute-start.5
  28.6 1.5 %shard_map.61.once = f32[34,200,128]{2,1,0:T(8,128)S(1)} custom-call(f32[66,200,128]{2,1,0:T(8,128)S(1)} %get-tuple-element.30.field), custom_call_target="tpu_custom_call" | custom-call | bytes 8388608 | tf_op jit(solution)/shard_map/pallas_call | solution.py:281
  30.1 2.0 %sweep_again_high.1 = (f32[64,16,1024]{2,1,0:T(8,128)}, f32[4096,128]{1,0:T(8,128)S(1)}) custom-call(f32[34,200,128]{2,1,0:T(8,128)S(1)} %shard_map.61.once, f32[32,16,1024]{2,1,0:T(8,128)S(1)} %get-tuple-element.39.low), custom_call_target="tpu_custom_call" | custom-call | bytes 8388608 | tf_op jit(solution)/shard_map/sweep_again_high/pallas_call | solution.py:350
  32.1 0.0 collective-permute-done.5.more
  32.1 0.0 collective-permute-done.first
  32.2 0.0 collective-permute-done.1.second
  32.2 0.1 collective-permute-start.8
  32.3 4.7 %collective-permute-start.9 = (f32[8,1024]{1,0:T(8,128)S(1)}, f32[8,1024]{1,0:T(8,128)S(1)}, u32[]{:S(2)}, u32[]{:S(2)}) collective-permute-start(f32[8,1024]{1,0:T(8,128)S(1)} %get-tuple-element.47), channel_id=1, source_target_pairs={{0,7},{1,0},{2,1},{3,2},{4,3},{5,4},{6,5},{7,6},{8,15},{9,8},{10,9... | collective-permute-start | bytes 98312 | tf_op jit(solution)/shard_map/ppermute | solution.py:528
  37.0 0.8 %patch_z.1 = (f32[64,16,1024]{2,1,0:T(8,128)}, f32[4,64,1024]{2,1,0:T(8,128)S(1)}) custom-call(f32[32,1024]{1,0:T(8,128)S(1)} %collective-permute-done.first, f32[32,1024]{1,0:T(8,128)S(1)} %collective-permute-done.1.second, f32[4096,128]{1,0:T(8,128)S(1)} %get-tuple-element.33.slab_low, ...), custom_call_target="tpu_custom_call", output_to_operand_aliasing={{0}: (4, {})} | custom-call | bytes 1048576 | tf_op jit(solution)/shard_map/patch_z/pallas_call | solution.py:438
  37.7 1.9 %collective-permute-done.8.clow = f32[8,1024]{1,0:T(8,128)S(1)} collective-permute-done((f32[8,1024]{1,0:T(8,128)S(1)}, f32[8,1024]{1,0:T(8,128)S(1)}, u32[]{:S(2)}, u32[]{:S(2)}) %collective-permute-start.8) | collective-permute-done | bytes 32800 | tf_op jit(solution)/shard_map/ppermute | solution.py:528
  39.6 1.0 %collective-permute-done.9.chigh = f32[8,1024]{1,0:T(8,128)S(1)} collective-permute-done((f32[8,1024]{1,0:T(8,128)S(1)}, f32[8,1024]{1,0:T(8,128)S(1)}, u32[]{:S(2)}, u32[]{:S(2)}) %collective-permute-start.9) | collective-permute-done | bytes 32800 | tf_op jit(solution)/shard_map/ppermute | solution.py:528
  40.7 0.0 collective-permute-done.6.near
  40.7 0.0 collective-permute-done.7.far
  40.7 1.6 %patch_far.1 = (f32[64,16,1024]{2,1,0:T(8,128)}, f32[1,1]{1,0:T(1,128)}) custom-call(f32[4,64,1024]{2,1,0:T(8,128)S(1)} %get-tuple-element.43.edges, f32[2,64,1024]{2,1,0:T(8,128)S(1)} %collective-permute-done.6.near, f32[2,64,1024]{2,1,0:T(8,128)S(1)} %collective-permute-done.7.far, ...), custom_call_target="tpu_custom_call", output_to_operand_aliasing={{0}: (6, {})} | custom-call | bytes 1048576 | tf_op jit(solution)/shard_map/patch_far/pallas_call | solution.py:507
  (4 shorter events, 0.0 us)
Async XLA Ops:
  6.9 6.4 %collective-permute-start.2 = (f32[8,1024]{1,0:T(8,128)S(1)}, f32[8,1024]{1,0:T(8,128)S(1)}, u32[]{:S(2)}, u32[]{:S(2)}) collective-permute-start(f32[8,1024]{1,0:T(8,128)S(1)} %get-tuple-element.29), channel_id=1, source_target_pairs={{0,4},{1,5},{2,6},{3,7},{4,0},{5,1},{6,2},{7,3},{8,12},{9,13},{10,... | collective-permute-start | bytes 98312 | tf_op jit(solution)/shard_map/ppermute | solution.py:528
  13.3 5.5 %collective-permute-start.3 = (f32[8,1024]{1,0:T(8,128)S(1)}, f32[8,1024]{1,0:T(8,128)S(1)}, u32[]{:S(2)}, u32[]{:S(2)}) collective-permute-start(f32[8,1024]{1,0:T(8,128)S(1)} %add.9), channel_id=1, source_target_pairs={{0,2},{1,3},{2,0},{3,1},{4,6},{5,7},{6,4},{7,5},{8,10},{9,11},{10,... | collective-permute-start | bytes 98312 | tf_op jit(solution)/shard_map/ppermute | solution.py:528
  15.7 25.0 %collective-permute-start.6 = (f32[2,64,1024]{2,1,0:T(8,128)S(1)}, f32[2,64,1024]{2,1,0:T(8,128)S(1)}, u32[]{:S(2)}, u32[]{:S(2)}) collective-permute-start(f32[2,64,1024]{2,1,0:T(8,128)S(1)} %shard_map.62), channel_id=1, source_target_pairs={{0,1},{1,0},{2,3},{3,2},{4,5},{5,4},{6,7},{7,6},{8,9},{9,8},{10,11... | collective-permute-start | bytes 1572872 | tf_op jit(solution)/shard_map/ppermute | solution.py:528
  18.8 22.0 %collective-permute-start.7 = (f32[2,64,1024]{2,1,0:T(8,128)S(1)}, f32[2,64,1024]{2,1,0:T(8,128)S(1)}, u32[]{:S(2)}, u32[]{:S(2)}) collective-permute-start(f32[2,64,1024]{2,1,0:T(8,128)S(1)} %shard_map.59), channel_id=1, source_target_pairs={{0,7},{1,2},{2,1},{3,4},{4,3},{5,6},{6,5},{7,0},{8,15},{9,10},{10,... | collective-permute-start | bytes 1572872 | tf_op jit(solution)/shard_map/ppermute | solution.py:528
  22.0 10.2 %collective-permute-start = (f32[32,1024]{1,0:T(8,128)S(1)}, f32[32,1024]{1,0:T(8,128)S(1)}, u32[]{:S(2)}, u32[]{:S(2)}) collective-permute-start(f32[32,1024]{1,0:T(8,128)S(1)} %get-tuple-element.27), channel_id=1, source_target_pairs={{0,24},{8,16},{16,8},{24,0},{1,25},{9,17},{17,9},{25,1},{2,26},{10... | collective-permute-start | bytes 393224 | tf_op jit(solution)/shard_map/ppermute | solution.py:528
  22.0 10.2 %collective-permute-start.1 = (f32[32,1024]{1,0:T(8,128)S(1)}, f32[32,1024]{1,0:T(8,128)S(1)}, u32[]{:S(2)}, u32[]{:S(2)}) collective-permute-start(f32[32,1024]{1,0:T(8,128)S(1)} %get-tuple-element.28), channel_id=1, source_target_pairs={{0,8},{8,0},{16,24},{24,16},{1,9},{9,1},{17,25},{25,17},{2,10},{10... | collective-permute-start | bytes 393224 | tf_op jit(solution)/shard_map/ppermute | solution.py:528
  23.6 4.8 %collective-permute-start.4 = (f32[8,1024]{1,0:T(8,128)S(1)}, f32[8,1024]{1,0:T(8,128)S(1)}, u32[]{:S(2)}, u32[]{:S(2)}) collective-permute-start(f32[8,1024]{1,0:T(8,128)S(1)} %add.10), channel_id=1, source_target_pairs={{0,24},{8,16},{16,8},{24,0},{1,25},{9,17},{17,9},{25,1},{2,26},{10... | collective-permute-start | bytes 98312 | tf_op jit(solution)/shard_map/ppermute | solution.py:528
  28.4 3.7 %collective-permute-start.5 = (f32[8,1024]{1,0:T(8,128)S(1)}, f32[8,1024]{1,0:T(8,128)S(1)}, u32[]{:S(2)}, u32[]{:S(2)}) collective-permute-start(f32[8,1024]{1,0:T(8,128)S(1)} %add.11.counts), channel_id=1, source_target_pairs={{0,8},{8,0},{16,24},{24,16},{1,9},{9,1},{17,25},{25,17},{2,10},{10... | collective-permute-start | bytes 98312 | tf_op jit(solution)/shard_map/ppermute | solution.py:528
  32.2 7.5 %collective-permute-start.8 = (f32[8,1024]{1,0:T(8,128)S(1)}, f32[8,1024]{1,0:T(8,128)S(1)}, u32[]{:S(2)}, u32[]{:S(2)}) collective-permute-start(f32[8,1024]{1,0:T(8,128)S(1)} %get-tuple-element.46), channel_id=1, source_target_pairs={{0,1},{1,2},{2,3},{3,4},{4,5},{5,6},{6,7},{7,0},{8,9},{9,10},{10,1... | collective-permute-start | bytes 98312 | tf_op jit(solution)/shard_map/ppermute | solution.py:528
  32.3 8.4 %collective-permute-start.9 = (f32[8,1024]{1,0:T(8,128)S(1)}, f32[8,1024]{1,0:T(8,128)S(1)}, u32[]{:S(2)}, u32[]{:S(2)}) collective-permute-start(f32[8,1024]{1,0:T(8,128)S(1)} %get-tuple-element.47), channel_id=1, source_target_pairs={{0,7},{1,0},{2,1},{3,2},{4,3},{5,4},{6,5},{7,6},{8,15},{9,8},{10,9... | collective-permute-start | bytes 98312 | tf_op jit(solution)/shard_map/ppermute | solution.py:528
